TPU v7x, 512 devices: a whole 4x4x16 slice. The times are simulated.
512 devices in a mesh: sec: 16 (over z_hi, y, core), gx: 32 (over x, z_lo).
Axes of the slice: x: 4, y: 4, z: 16 (z_hi: 2, z_lo: 8; z = z_hi * 8 + z_lo), core: 2. Of those that a mesh axis runs over, the one named last changes fastest.
Arguments:
- incoming: float32 [16, 128, 64, 256], P('sec', 'gx'), may hold values from 0.5 to 2
- backward: bfloat16 [64, 128, 64, 256], P('sec', 'gx'), may hold values from 0.5 to 2
- fields: float32 [3, 128, 256], P(None, 'gx'), may hold values from -0.4 to 0.4
- block_types: int32 [16, 4], P('sec'), may hold values from 0 to 2
- axial_taps: float32 [3, 64], replicated, may hold values from 0.1 to 0.45
- lateral_taps: float32 [3, 64], replicated, may hold values from 0.1 to 0.45
- depth_taps: float32 [3, 64], replicated, may hold values from 0.1 to 0.45
- bend_diagonal: float32 [64], replicated, may hold values from 0.4 to 0.8
- bend_coupling: float32 [64, 64], replicated, may hold values from 0 to 0.025
Outputs:
- handoff: float32 [16, 128, 64, 256], P('sec', 'gx')
- density: float32 [128, 64, 256], P('gx', 'sec')
All inputs are finite; a program needn't handle non-finite values.
Results may differ from a plain program's by a relative error of at most 0.0003.
Values sent between devices are 32-bit elements; how exact they have to be, the bound alone decides.
A program may use at most 64 MiB of HBM per device.

v0:
```python
import jax
import jax.numpy as jnp
from jax import lax
from jax.sharding import PartitionSpec as P

TICKS = 3
CZ = 64


def padded_2(block, sides, width):
    for axis, dim in sides:
        count = lax.axis_size(axis)
        forward = [(i, i + 1) for i in range(count - 1)]
        forward.append((count - 1, 0))
        backward = [(target, source) for source, target in forward]
        low = lax.ppermute(
            lax.slice_in_dim(block, block.shape[dim] - width, None, axis=dim), axis, forward
        )
        high = lax.ppermute(lax.slice_in_dim(block, 0, width, axis=dim), axis, backward)
        block = jnp.concatenate([low, block, high], axis=dim)
    return block


def from_behind(array, axis, by):
    length = lax.axis_size(axis)
    pairs = [(i, i + by) for i in range(length) if 0 <= i + by < length]
    return lax.ppermute(array, axis, pairs)


def boltzmann(fields, kinds):
    selector = kinds == jnp.arange(fields.shape[0], dtype=jnp.int32)
    chosen = jnp.sum(jnp.where(selector[:, None, None], fields, jnp.zeros_like(fields)), axis=0)
    return jnp.exp(-chosen)


def column(taps, which):
    return taps[which][None, :, None]


def advance_padded(padded, factor, axial_taps, lateral_taps, depth_taps, kernel):
    along_x = (
        column(axial_taps, 0) * padded[:-2]
        + column(axial_taps, 1) * padded[1:-1]
        + column(axial_taps, 2) * padded[2:]
    )
    along_y = (
        column(lateral_taps, 0) * jnp.roll(along_x, CZ, axis=2)
        + column(lateral_taps, 1) * along_x
        + column(lateral_taps, 2) * jnp.roll(along_x, -CZ, axis=2)
    )
    depth_pos = (jnp.arange(along_y.shape[2], dtype=jnp.int32) % CZ)[None, None, :]
    behind = jnp.where(
        depth_pos == 0, jnp.roll(along_y, -(CZ - 1), axis=2), jnp.roll(along_y, 1, axis=2)
    )
    ahead = jnp.where(
        depth_pos == CZ - 1, jnp.roll(along_y, CZ - 1, axis=2), jnp.roll(along_y, -1, axis=2)
    )
    along_z = (
        column(depth_taps, 0) * behind
        + column(depth_taps, 1) * along_y
        + column(depth_taps, 2) * ahead
    )
    blended = jnp.einsum(
        "uv,xvc->xuc",
        kernel,
        along_z,
        precision=lax.Precision.HIGHEST,
        preferred_element_type=jnp.float32,
    )
    return blended * factor[:, None, :]


def per_device(
    incoming,
    backward,
    fields,
    block_types,
    axial_taps,
    lateral_taps,
    depth_taps,
    bend_diagonal,
    bend_coupling,
):
    kernel = jnp.diag(bend_diagonal) + bend_coupling
    steps_each = block_types.shape[1]
    start = incoming[0]
    first_section = lax.axis_index("sec") == 0
    factors = [boltzmann(fields, block_types[0, position]) for position in range(steps_each)]
    current = start
    outgoing = start
    accumulated = jnp.zeros(start.shape, jnp.float32)
    for tick_index in range(TICKS):
        final_tick = tick_index + 1 == TICKS
        propagator = current
        for position in range(steps_each):
            padded = padded_2(propagator, (("gx", 0),), 1)
            propagator = advance_padded(
                padded, factors[position], axial_taps, lateral_taps, depth_taps, kernel
            )
            if final_tick:
                accumulated = accumulated + propagator * backward[position].astype(jnp.float32)
        outgoing = propagator
        if not final_tick:
            shifted = from_behind(outgoing, "sec", 1)
            current = jnp.where(first_section, start, shifted)
    reduced = lax.psum_scatter(accumulated, "sec", scatter_dimension=1, tiled=True)
    density = reduced / (lax.axis_size("sec") * steps_each)
    return (outgoing[None], density)


def solution(mesh):
    in_specs = (
        P("sec", "gx", None, None),
        P("sec", "gx", None, None),
        P(None, "gx", None),
        P("sec", None),
        P(),
        P(),
        P(),
        P(),
        P(),
    )
    out_specs = (P("sec", "gx", None, None), P("gx", "sec", None))
    return jax.shard_map(
        per_device, mesh=mesh, in_specs=in_specs, out_specs=out_specs, check_vma=False
    )
```

profile of v0, /device:TPU:1, one launch (start us, length us, event | category | flops | bytes accessed | tf_op | source)
XLA Modules:
  0.0 552.3 jit_solution(8789117345770059605)
XLA Ops:
  8.2 4.4 collective-permute-start
  12.5 13.4 %collective-permute-start.1 = (f32[1,64,256]{2,1,0:T(8,128)S(1)}, f32[1,64,256]{2,1,0:T(8,128)S(1)}, u32[]{:S(2)}, u32[]{:S(2)}) collective-permute-start(f32[1,64,256]{2,1,0:T(8,128)S(1)} %get-tuple-element.173), channel_id=1, source_target_pairs={{1,0},{2,1},{3,2},{4,3},{5,4},{6,5},{7,6},{8,7},{9,8},{10,9},{11,1... | collective-permute-start | bytes 196616 | tf_op jit(solution)/shard_map/ppermute | solution.py:19
  35.1 12.1 %collective-permute-start.3 = (f32[1,64,256]{2,1,0:T(8,128)S(1)}, f32[1,64,256]{2,1,0:T(8,128)S(1)}, u32[]{:S(2)}, u32[]{:S(2)}) collective-permute-start(f32[1,64,256]{2,1,0:T(8,128)S(1)} %get-tuple-element.159), channel_id=1, source_target_pairs={{1,0},{2,1},{3,2},{4,3},{5,4},{6,5},{7,6},{8,7},{9,8},{10,9},{11,1... | collective-permute-start | bytes 196616 | tf_op jit(solution)/shard_map/ppermute | solution.py:19
  50.3 1.9 collective-permute-start.4
  52.2 12.5 %collective-permute-start.5 = (f32[1,64,256]{2,1,0:T(8,128)S(1)}, f32[1,64,256]{2,1,0:T(8,128)S(1)}, u32[]{:S(2)}, u32[]{:S(2)}) collective-permute-start(f32[1,64,256]{2,1,0:T(8,128)S(1)} %get-tuple-element.145), channel_id=1, source_target_pairs={{1,0},{2,1},{3,2},{4,3},{5,4},{6,5},{7,6},{8,7},{9,8},{10,9},{11,1... | collective-permute-start | bytes 196616 | tf_op jit(solution)/shard_map/ppermute | solution.py:19
  69.7 12.4 %collective-permute-start.7 = (f32[1,64,256]{2,1,0:T(8,128)S(1)}, f32[1,64,256]{2,1,0:T(8,128)S(1)}, u32[]{:S(2)}, u32[]{:S(2)}) collective-permute-start(f32[1,64,256]{2,1,0:T(8,128)S(1)} %get-tuple-element.131), channel_id=1, source_target_pairs={{1,0},{2,1},{3,2},{4,3},{5,4},{6,5},{7,6},{8,7},{9,8},{10,9},{11,1... | collective-permute-start | bytes 196616 | tf_op jit(solution)/shard_map/ppermute | solution.py:19
  85.3 7.4 %collective-permute-start.8 = (f32[4,64,256]{2,1,0:T(8,128)S(1)}, f32[4,64,256]{2,1,0:T(8,128)S(1)}, u32[]{:S(2)}, u32[]{:S(2)}) collective-permute-start(f32[4,64,256]{2,1,0:T(8,128)S(1)} %fusion.7), channel_id=1, source_target_pairs={{0,32},{32,64},{64,96},{96,128},{128,160},{160,192},{192,224},{224... | collective-permute-start | bytes 786440 | tf_op jit(solution)/shard_map/ppermute | solution.py:27
  92.7 3.3 collective-permute-done.8
  96.0 12.7 %collective-permute-start.10 = (f32[1,64,256]{2,1,0:T(8,128)S(1)}, f32[1,64,256]{2,1,0:T(8,128)S(1)}, u32[]{:S(2)}, u32[]{:S(2)}) collective-permute-start(f32[1,64,256]{2,1,0:T(8,128)S(1)} %get-tuple-element.117), channel_id=1, source_target_pairs={{1,0},{2,1},{3,2},{4,3},{5,4},{6,5},{7,6},{8,7},{9,8},{10,9},{11,1... | collective-permute-start | bytes 196616 | tf_op jit(solution)/shard_map/ppermute | solution.py:19
  108.7 1.9 collective-permute-start.9
  110.7 12.4 %collective-permute-done.9 = f32[1,64,256]{2,1,0:T(8,128)S(1)} collective-permute-done((f32[1,64,256]{2,1,0:T(8,128)S(1)}, f32[1,64,256]{2,1,0:T(8,128)S(1)}, u32[]{:S(2)}, u32[]{:S(2)}) %collective-permute-start.9) | collective-permute-done | bytes 65568 | tf_op jit(solution)/shard_map/ppermute | solution.py:16
  124.8 1.9 collective-permute-start.11
  126.7 12.1 %collective-permute-start.12 = (f32[1,64,256]{2,1,0:T(8,128)S(1)}, f32[1,64,256]{2,1,0:T(8,128)S(1)}, u32[]{:S(2)}, u32[]{:S(2)}) collective-permute-start(f32[1,64,256]{2,1,0:T(8,128)S(1)} %get-tuple-element.103), channel_id=1, source_target_pairs={{1,0},{2,1},{3,2},{4,3},{5,4},{6,5},{7,6},{8,7},{9,8},{10,9},{11,1... | collective-permute-start | bytes 196616 | tf_op jit(solution)/shard_map/ppermute | solution.py:19
  143.8 12.4 %collective-permute-start.14 = (f32[1,64,256]{2,1,0:T(8,128)S(1)}, f32[1,64,256]{2,1,0:T(8,128)S(1)}, u32[]{:S(2)}, u32[]{:S(2)}) collective-permute-start(f32[1,64,256]{2,1,0:T(8,128)S(1)} %get-tuple-element.89), channel_id=1, source_target_pairs={{1,0},{2,1},{3,2},{4,3},{5,4},{6,5},{7,6},{8,7},{9,8},{10,9},{11,1... | collective-permute-start | bytes 196616 | tf_op jit(solution)/shard_map/ppermute | solution.py:19
  161.3 12.4 %collective-permute-start.16 = (f32[1,64,256]{2,1,0:T(8,128)S(1)}, f32[1,64,256]{2,1,0:T(8,128)S(1)}, u32[]{:S(2)}, u32[]{:S(2)}) collective-permute-start(f32[1,64,256]{2,1,0:T(8,128)S(1)} %get-tuple-element.75), channel_id=1, source_target_pairs={{1,0},{2,1},{3,2},{4,3},{5,4},{6,5},{7,6},{8,7},{9,8},{10,9},{11,1... | collective-permute-start | bytes 196616 | tf_op jit(solution)/shard_map/ppermute | solution.py:19
  176.7 9.1 %collective-permute-start.17 = (f32[4,64,256]{2,1,0:T(8,128)S(1)}, f32[4,64,256]{2,1,0:T(8,128)S(1)}, u32[]{:S(2)}, u32[]{:S(2)}) collective-permute-start(f32[4,64,256]{2,1,0:T(8,128)S(1)} %fusion.3), channel_id=1, source_target_pairs={{0,32},{32,64},{64,96},{96,128},{128,160},{160,192},{192,224},{224... | collective-permute-start | bytes 786440 | tf_op jit(solution)/shard_map/ppermute | solution.py:27
  185.9 3.3 collective-permute-done.17
  191.1 12.9 %collective-permute-start.19 = (f32[1,64,256]{2,1,0:T(8,128)S(1)}, f32[1,64,256]{2,1,0:T(8,128)S(1)}, u32[]{:S(2)}, u32[]{:S(2)}) collective-permute-start(f32[1,64,256]{2,1,0:T(8,128)S(1)} %get-tuple-element.61), channel_id=1, source_target_pairs={{1,0},{2,1},{3,2},{4,3},{5,4},{6,5},{7,6},{8,7},{9,8},{10,9},{11,1... | collective-permute-start | bytes 196616 | tf_op jit(solution)/shard_map/ppermute | solution.py:19
  209.4 12.5 %collective-permute-start.21 = (f32[1,64,256]{2,1,0:T(8,128)S(1)}, f32[1,64,256]{2,1,0:T(8,128)S(1)}, u32[]{:S(2)}, u32[]{:S(2)}) collective-permute-start(f32[1,64,256]{2,1,0:T(8,128)S(1)} %get-tuple-element.47), channel_id=1, source_target_pairs={{1,0},{2,1},{3,2},{4,3},{5,4},{6,5},{7,6},{8,7},{9,8},{10,9},{11,1... | collective-permute-start | bytes 196616 | tf_op jit(solution)/shard_map/ppermute | solution.py:19
  227.0 12.5 %collective-permute-start.23 = (f32[1,64,256]{2,1,0:T(8,128)S(1)}, f32[1,64,256]{2,1,0:T(8,128)S(1)}, u32[]{:S(2)}, u32[]{:S(2)}) collective-permute-start(f32[1,64,256]{2,1,0:T(8,128)S(1)} %get-tuple-element.33), channel_id=1, source_target_pairs={{1,0},{2,1},{3,2},{4,3},{5,4},{6,5},{7,6},{8,7},{9,8},{10,9},{11,1... | collective-permute-start | bytes 196616 | tf_op jit(solution)/shard_map/ppermute | solution.py:19
  242.6 1.9 collective-permute-start.24
  244.5 12.4 %collective-permute-start.25 = (f32[1,64,256]{2,1,0:T(8,128)S(1)}, f32[1,64,256]{2,1,0:T(8,128)S(1)}, u32[]{:S(2)}, u32[]{:S(2)}) collective-permute-start(f32[1,64,256]{2,1,0:T(8,128)S(1)} %get-tuple-element.19), channel_id=1, source_target_pairs={{1,0},{2,1},{3,2},{4,3},{5,4},{6,5},{7,6},{8,7},{9,8},{10,9},{11,1... | collective-permute-start | bytes 196616 | tf_op jit(solution)/shard_map/ppermute | solution.py:19
  259.3 2.6 fusion.275
  263.9 280.2 %all-reduce.3.cloned.1.call-done = f32[4,64,256]{2,1,0:T(8,128)} async-done(((f32[4,64,256]{2,1,0:T(8,128)}), f32[4,64,256]{2,1,0:T(8,128)}) %all-reduce.3.cloned.1.call-update) | async-done | bytes 262160
  (183 shorter events, 55.5 us)
Async XLA Ops:
  7.2 536.9 %all-reduce.3.cloned.1.call-start = ((), (), s32[]{:S(2)}) async-start(), calls=%async_computation | async-start | bytes 524288
  8.2 22.5 %collective-permute-start = (f32[1,64,256]{2,1,0:T(8,128)S(1)}, f32[1,64,256]{2,1,0:T(8,128)S(1)}, u32[]{:S(2)}, u32[]{:S(2)}) collective-permute-start(f32[1,64,256]{2,1,0:T(8,128)S(1)} %get-tuple-element.172), channel_id=1, source_target_pairs={{0,1},{1,2},{2,3},{3,4},{4,5},{5,6},{6,7},{7,8},{8,9},{9,10},{10,1... | collective-permute-start | bytes 196616 | tf_op jit(solution)/shard_map/ppermute | solution.py:16
  12.5 18.2 %collective-permute-start.1 = (f32[1,64,256]{2,1,0:T(8,128)S(1)}, f32[1,64,256]{2,1,0:T(8,128)S(1)}, u32[]{:S(2)}, u32[]{:S(2)}) collective-permute-start(f32[1,64,256]{2,1,0:T(8,128)S(1)} %get-tuple-element.173), channel_id=1, source_target_pairs={{1,0},{2,1},{3,2},{4,3},{5,4},{6,5},{7,6},{8,7},{9,8},{10,9},{11,1... | collective-permute-start | bytes 196616 | tf_op jit(solution)/shard_map/ppermute | solution.py:19
  33.2 14.0 %collective-permute-start.2 = (f32[1,64,256]{2,1,0:T(8,128)S(1)}, f32[1,64,256]{2,1,0:T(8,128)S(1)}, u32[]{:S(2)}, u32[]{:S(2)}) collective-permute-start(f32[1,64,256]{2,1,0:T(8,128)S(1)} %get-tuple-element.158), channel_id=1, source_target_pairs={{0,1},{1,2},{2,3},{3,4},{4,5},{5,6},{6,7},{7,8},{8,9},{9,10},{10,1... | collective-permute-start | bytes 196616 | tf_op jit(solution)/shard_map/ppermute | solution.py:16
  50.3 14.5 %collective-permute-start.4 = (f32[1,64,256]{2,1,0:T(8,128)S(1)}, f32[1,64,256]{2,1,0:T(8,128)S(1)}, u32[]{:S(2)}, u32[]{:S(2)}) collective-permute-start(f32[1,64,256]{2,1,0:T(8,128)S(1)} %get-tuple-element.144), channel_id=1, source_target_pairs={{0,1},{1,2},{2,3},{3,4},{4,5},{5,6},{6,7},{7,8},{8,9},{9,10},{10,1... | collective-permute-start | bytes 196616 | tf_op jit(solution)/shard_map/ppermute | solution.py:16
  52.2 13.8 %collective-permute-start.5 = (f32[1,64,256]{2,1,0:T(8,128)S(1)}, f32[1,64,256]{2,1,0:T(8,128)S(1)}, u32[]{:S(2)}, u32[]{:S(2)}) collective-permute-start(f32[1,64,256]{2,1,0:T(8,128)S(1)} %get-tuple-element.145), channel_id=1, source_target_pairs={{1,0},{2,1},{3,2},{4,3},{5,4},{6,5},{7,6},{8,7},{9,8},{10,9},{11,1... | collective-permute-start | bytes 196616 | tf_op jit(solution)/shard_map/ppermute | solution.py:19
  67.8 14.4 %collective-permute-start.6 = (f32[1,64,256]{2,1,0:T(8,128)S(1)}, f32[1,64,256]{2,1,0:T(8,128)S(1)}, u32[]{:S(2)}, u32[]{:S(2)}) collective-permute-start(f32[1,64,256]{2,1,0:T(8,128)S(1)} %get-tuple-element.130), channel_id=1, source_target_pairs={{0,1},{1,2},{2,3},{3,4},{4,5},{5,6},{6,7},{7,8},{8,9},{9,10},{10,1... | collective-permute-start | bytes 196616 | tf_op jit(solution)/shard_map/ppermute | solution.py:16
  69.7 13.8 %collective-permute-start.7 = (f32[1,64,256]{2,1,0:T(8,128)S(1)}, f32[1,64,256]{2,1,0:T(8,128)S(1)}, u32[]{:S(2)}, u32[]{:S(2)}) collective-permute-start(f32[1,64,256]{2,1,0:T(8,128)S(1)} %get-tuple-element.131), channel_id=1, source_target_pairs={{1,0},{2,1},{3,2},{4,3},{5,4},{6,5},{7,6},{8,7},{9,8},{10,9},{11,1... | collective-permute-start | bytes 196616 | tf_op jit(solution)/shard_map/ppermute | solution.py:19
  96.0 14.7 %collective-permute-start.10 = (f32[1,64,256]{2,1,0:T(8,128)S(1)}, f32[1,64,256]{2,1,0:T(8,128)S(1)}, u32[]{:S(2)}, u32[]{:S(2)}) collective-permute-start(f32[1,64,256]{2,1,0:T(8,128)S(1)} %get-tuple-element.117), channel_id=1, source_target_pairs={{1,0},{2,1},{3,2},{4,3},{5,4},{6,5},{7,6},{8,7},{9,8},{10,9},{11,1... | collective-permute-start | bytes 196616 | tf_op jit(solution)/shard_map/ppermute | solution.py:19
  108.7 14.3 %collective-permute-start.9 = (f32[1,64,256]{2,1,0:T(8,128)S(1)}, f32[1,64,256]{2,1,0:T(8,128)S(1)}, u32[]{:S(2)}, u32[]{:S(2)}) collective-permute-start(f32[1,64,256]{2,1,0:T(8,128)S(1)} %get-tuple-element.116), channel_id=1, source_target_pairs={{0,1},{1,2},{2,3},{3,4},{4,5},{5,6},{6,7},{7,8},{8,9},{9,10},{10,1... | collective-permute-start | bytes 196616 | tf_op jit(solution)/shard_map/ppermute | solution.py:16
  124.8 14.0 %collective-permute-start.11 = (f32[1,64,256]{2,1,0:T(8,128)S(1)}, f32[1,64,256]{2,1,0:T(8,128)S(1)}, u32[]{:S(2)}, u32[]{:S(2)}) collective-permute-start(f32[1,64,256]{2,1,0:T(8,128)S(1)} %get-tuple-element.102), channel_id=1, source_target_pairs={{0,1},{1,2},{2,3},{3,4},{4,5},{5,6},{6,7},{7,8},{8,9},{9,10},{10,1... | collective-permute-start | bytes 196616 | tf_op jit(solution)/shard_map/ppermute | solution.py:16
  126.7 13.4 %collective-permute-start.12 = (f32[1,64,256]{2,1,0:T(8,128)S(1)}, f32[1,64,256]{2,1,0:T(8,128)S(1)}, u32[]{:S(2)}, u32[]{:S(2)}) collective-permute-start(f32[1,64,256]{2,1,0:T(8,128)S(1)} %get-tuple-element.103), channel_id=1, source_target_pairs={{1,0},{2,1},{3,2},{4,3},{5,4},{6,5},{7,6},{8,7},{9,8},{10,9},{11,1... | collective-permute-start | bytes 196616 | tf_op jit(solution)/shard_map/ppermute | solution.py:19
  141.9 14.3 %collective-permute-start.13 = (f32[1,64,256]{2,1,0:T(8,128)S(1)}, f32[1,64,256]{2,1,0:T(8,128)S(1)}, u32[]{:S(2)}, u32[]{:S(2)}) collective-permute-start(f32[1,64,256]{2,1,0:T(8,128)S(1)} %get-tuple-element.88), channel_id=1, source_target_pairs={{0,1},{1,2},{2,3},{3,4},{4,5},{5,6},{6,7},{7,8},{8,9},{9,10},{10,1... | collective-permute-start | bytes 196616 | tf_op jit(solution)/shard_map/ppermute | solution.py:16
  143.8 13.7 %collective-permute-start.14 = (f32[1,64,256]{2,1,0:T(8,128)S(1)}, f32[1,64,256]{2,1,0:T(8,128)S(1)}, u32[]{:S(2)}, u32[]{:S(2)}) collective-permute-start(f32[1,64,256]{2,1,0:T(8,128)S(1)} %get-tuple-element.89), channel_id=1, source_target_pairs={{1,0},{2,1},{3,2},{4,3},{5,4},{6,5},{7,6},{8,7},{9,8},{10,9},{11,1... | collective-permute-start | bytes 196616 | tf_op jit(solution)/shard_map/ppermute | solution.py:19
  159.3 14.3 %collective-permute-start.15 = (f32[1,64,256]{2,1,0:T(8,128)S(1)}, f32[1,64,256]{2,1,0:T(8,128)S(1)}, u32[]{:S(2)}, u32[]{:S(2)}) collective-permute-start(f32[1,64,256]{2,1,0:T(8,128)S(1)} %get-tuple-element.74), channel_id=1, source_target_pairs={{0,1},{1,2},{2,3},{3,4},{4,5},{5,6},{6,7},{7,8},{8,9},{9,10},{10,1... | collective-permute-start | bytes 196616 | tf_op jit(solution)/shard_map/ppermute | solution.py:16
  161.3 13.7 %collective-permute-start.16 = (f32[1,64,256]{2,1,0:T(8,128)S(1)}, f32[1,64,256]{2,1,0:T(8,128)S(1)}, u32[]{:S(2)}, u32[]{:S(2)}) collective-permute-start(f32[1,64,256]{2,1,0:T(8,128)S(1)} %get-tuple-element.75), channel_id=1, source_target_pairs={{1,0},{2,1},{3,2},{4,3},{5,4},{6,5},{7,6},{8,7},{9,8},{10,9},{11,1... | collective-permute-start | bytes 196616 | tf_op jit(solution)/shard_map/ppermute | solution.py:19
  189.2 14.8 %collective-permute-start.18 = (f32[1,64,256]{2,1,0:T(8,128)S(1)}, f32[1,64,256]{2,1,0:T(8,128)S(1)}, u32[]{:S(2)}, u32[]{:S(2)}) collective-permute-start(f32[1,64,256]{2,1,0:T(8,128)S(1)} %get-tuple-element.60), channel_id=1, source_target_pairs={{0,1},{1,2},{2,3},{3,4},{4,5},{5,6},{6,7},{7,8},{8,9},{9,10},{10,1... | collective-permute-start | bytes 196616 | tf_op jit(solution)/shard_map/ppermute | solution.py:16
  191.1 14.6 %collective-permute-start.19 = (f32[1,64,256]{2,1,0:T(8,128)S(1)}, f32[1,64,256]{2,1,0:T(8,128)S(1)}, u32[]{:S(2)}, u32[]{:S(2)}) collective-permute-start(f32[1,64,256]{2,1,0:T(8,128)S(1)} %get-tuple-element.61), channel_id=1, source_target_pairs={{1,0},{2,1},{3,2},{4,3},{5,4},{6,5},{7,6},{8,7},{9,8},{10,9},{11,1... | collective-permute-start | bytes 196616 | tf_op jit(solution)/shard_map/ppermute | solution.py:19
  207.5 14.5 %collective-permute-start.20 = (f32[1,64,256]{2,1,0:T(8,128)S(1)}, f32[1,64,256]{2,1,0:T(8,128)S(1)}, u32[]{:S(2)}, u32[]{:S(2)}) collective-permute-start(f32[1,64,256]{2,1,0:T(8,128)S(1)} %get-tuple-element.46), channel_id=1, source_target_pairs={{0,1},{1,2},{2,3},{3,4},{4,5},{5,6},{6,7},{7,8},{8,9},{9,10},{10,1... | collective-permute-start | bytes 196616 | tf_op jit(solution)/shard_map/ppermute | solution.py:16
  209.4 13.8 %collective-permute-start.21 = (f32[1,64,256]{2,1,0:T(8,128)S(1)}, f32[1,64,256]{2,1,0:T(8,128)S(1)}, u32[]{:S(2)}, u32[]{:S(2)}) collective-permute-start(f32[1,64,256]{2,1,0:T(8,128)S(1)} %get-tuple-element.47), channel_id=1, source_target_pairs={{1,0},{2,1},{3,2},{4,3},{5,4},{6,5},{7,6},{8,7},{9,8},{10,9},{11,1... | collective-permute-start | bytes 196616 | tf_op jit(solution)/shard_map/ppermute | solution.py:19
  225.0 14.8 %collective-permute-start.22 = (f32[1,64,256]{2,1,0:T(8,128)S(1)}, f32[1,64,256]{2,1,0:T(8,128)S(1)}, u32[]{:S(2)}, u32[]{:S(2)}) collective-permute-start(f32[1,64,256]{2,1,0:T(8,128)S(1)} %get-tuple-element.32), channel_id=1, source_target_pairs={{0,1},{1,2},{2,3},{3,4},{4,5},{5,6},{6,7},{7,8},{8,9},{9,10},{10,1... | collective-permute-start | bytes 196616 | tf_op jit(solution)/shard_map/ppermute | solution.py:16
  227.0 13.8 %collective-permute-start.23 = (f32[1,64,256]{2,1,0:T(8,128)S(1)}, f32[1,64,256]{2,1,0:T(8,128)S(1)}, u32[]{:S(2)}, u32[]{:S(2)}) collective-permute-start(f32[1,64,256]{2,1,0:T(8,128)S(1)} %get-tuple-element.33), channel_id=1, source_target_pairs={{1,0},{2,1},{3,2},{4,3},{5,4},{6,5},{7,6},{8,7},{9,8},{10,9},{11,1... | collective-permute-start | bytes 196616 | tf_op jit(solution)/shard_map/ppermute | solution.py:19
  242.6 14.3 %collective-permute-start.24 = (f32[1,64,256]{2,1,0:T(8,128)S(1)}, f32[1,64,256]{2,1,0:T(8,128)S(1)}, u32[]{:S(2)}, u32[]{:S(2)}) collective-permute-start(f32[1,64,256]{2,1,0:T(8,128)S(1)} %get-tuple-element.18), channel_id=1, source_target_pairs={{0,1},{1,2},{2,3},{3,4},{4,5},{5,6},{6,7},{7,8},{8,9},{9,10},{10,1... | collective-permute-start | bytes 196616 | tf_op jit(solution)/shard_map/ppermute | solution.py:16
  244.5 13.7 %collective-permute-start.25 = (f32[1,64,256]{2,1,0:T(8,128)S(1)}, f32[1,64,256]{2,1,0:T(8,128)S(1)}, u32[]{:S(2)}, u32[]{:S(2)}) collective-permute-start(f32[1,64,256]{2,1,0:T(8,128)S(1)} %get-tuple-element.19), channel_id=1, source_target_pairs={{1,0},{2,1},{3,2},{4,3},{5,4},{6,5},{7,6},{8,7},{9,8},{10,9},{11,1... | collective-permute-start | bytes 196616 | tf_op jit(solution)/shard_map/ppermute | solution.py:19
  (11 other events, 101.1 us)
Sparse Core Ops, SparseCore 0:
  262.1 281.9 all-reduce.2
where the time goes:
time: 553 us; the launch traced here: 552 us
  waiting for transfers between devices  313 us (57%)
  starting transfers between devices  192 us (35%)
  between operations  16 us (3%)
  local copies, waits for them, and re-layouts  13.1 us (2%)
  matrix products  9.86 us (2%)
  other arithmetic  8.28 us (1%)
    unnamed x2, waiting for transfers between devices  280 us
    ppermute x12, starting transfers between devices, padded_2(): lax.ppermute(lax.slice_in_dim(block, 0, width, axis=dim), axis, backward)  150 us
    ppermute x12, starting transfers between devices, padded_2(): lax.ppermute(lax.slice_in_dim(block, block.shape[dim] - width, None, axis...  25.5 us
    ppermute x2, starting transfers between devices, from_behind(): return lax.ppermute(array, axis, pairs)  16.5 us
    ppermute x12, waiting for transfers between devices, padded_2(): lax.ppermute(lax.slice_in_dim(block, 0, width, axis=dim), axis, backward)  13 us
    ppermute x12, waiting for transfers between devices, padded_2(): lax.ppermute(lax.slice_in_dim(block, block.shape[dim] - width, None, axis...  12.7 us
  transfers between devices with their start and end apart: 27, of which 15 were waited for; matrix products, arithmetic and copies ran while one was open for 1% of the time, Pallas kernels for 0%

commit v1 on v0

v1 whole, which is shorter than its diff:
```python
import functools

import jax
import jax.numpy as jnp
from jax import lax
from jax.experimental import pallas as pl
from jax.experimental.pallas import tpu as pltpu
from jax.sharding import PartitionSpec as P

MESH = pl.DeviceIdType.MESH
PLANES = 4
LEVELS = 12
SPAN = PLANES + 2 * LEVELS
OWN = LEVELS
ORIENT = 64
CELLS = 256


def body(
    n_gx, contour,
    inc, back, fld, btr, taps, kmat,
    hand, den,
    lev, fw, bt, part, summed, kcat, r_core, r_y, s_y, r_z,
    mv_send, mv_recv, mv_extra, h_send, h_recv, f_send, f_recv, b_send, b_recv,
    loc, c_send, c_recv, y_send, y_recv, z_send, z_recv,
):
    k = lax.axis_index("sec")
    g = lax.axis_index("gx")
    core = lax.rem(k, 2)
    y = lax.rem(lax.div(k, 2), 4)
    zhi = lax.div(k, 8)
    right = lax.rem(g + 1, n_gx)
    left = lax.rem(g + n_gx - 1, n_gx)
    other_core = k + 1 - 2 * core
    other_z = lax.rem(k + 8, 16)

    def across(dy):
        return 8 * zhi + 2 * lax.rem(y + dy, 4) + core

    bt[pl.ds(0, 8)] = jnp.zeros((8, 1, CELLS), jnp.float32)
    barrier = pltpu.get_barrier_semaphore()
    sections = [lax.rem(k + n, 16) for n in (1, 2, 14, 15)]
    sections += [other_core, other_z] + [across(n) for n in (1, 2, 3)]
    for n in sections:
        pl.semaphore_signal(barrier, inc=1, device_id=(n, g), device_id_type=MESH)
    for n in (left, right):
        pl.semaphore_signal(barrier, inc=1, device_id=(k, n), device_id_type=MESH)

    own_fw = pltpu.make_async_copy(fld, fw.at[pl.ds(OWN, PLANES)], loc.at[0])
    own_bt = pltpu.make_async_copy(btr, bt.at[pl.ds(8, 4)], loc.at[1])
    own_fw.start()
    own_bt.start()
    full = kmat[...]
    high = full.astype(jnp.bfloat16)
    low = (full - high.astype(jnp.float32)).astype(jnp.bfloat16)
    col = lax.broadcasted_iota(jnp.int32, full.shape, 1)
    mixed = jnp.where(
        jnp.logical_and(col >= ORIENT, col < 2 * ORIENT), low.astype(jnp.float32), high.astype(jnp.float32)
    )
    kcat[...] = mixed.astype(jnp.bfloat16)
    own_fw.wait()
    own_bt.wait()

    pl.semaphore_wait(barrier, 11)

    def move(p, target, send, recv):
        return pltpu.make_async_remote_copy(
            src_ref=inc.at[p], dst_ref=lev.at[OWN + p], send_sem=send, recv_sem=recv,
            device_id=(target, g), device_id_type=MESH,
        )

    def halo_right(d):
        return pltpu.make_async_remote_copy(
            src_ref=lev.at[OWN + PLANES - d], dst_ref=lev.at[OWN - d],
            send_sem=h_send.at[0, d - 1], recv_sem=h_recv.at[0, d - 1],
            device_id=(k, right), device_id_type=MESH,
        )

    def halo_left(d):
        return pltpu.make_async_remote_copy(
            src_ref=lev.at[OWN - 1 + d], dst_ref=lev.at[OWN + PLANES - 1 + d],
            send_sem=h_send.at[1, d - 1], recv_sem=h_recv.at[1, d - 1],
            device_id=(k, left), device_id_type=MESH,
        )

    def field_right(r):
        return pltpu.make_async_remote_copy(
            src_ref=fw.at[pl.ds(OWN + PLANES - PLANES * r, PLANES)],
            dst_ref=fw.at[pl.ds(OWN - PLANES * r, PLANES)],
            send_sem=f_send.at[0, r - 1], recv_sem=f_recv.at[0, r - 1],
            device_id=(k, right), device_id_type=MESH,
        )

    def field_left(r):
        return pltpu.make_async_remote_copy(
            src_ref=fw.at[pl.ds(OWN - PLANES + PLANES * r, PLANES)],
            dst_ref=fw.at[pl.ds(OWN + PLANES * r, PLANES)],
            send_sem=f_send.at[1, r - 1], recv_sem=f_recv.at[1, r - 1],
            device_id=(k, left), device_id_type=MESH,
        )

    def kinds(ahead):
        return pltpu.make_async_remote_copy(
            src_ref=btr, dst_ref=bt.at[pl.ds(8 - 4 * ahead, 4)],
            send_sem=b_send.at[ahead - 1], recv_sem=b_recv.at[ahead - 1],
            device_id=(lax.rem(k + ahead, 16), g), device_id_type=MESH,
        )

    order = (3, 0, 2, 1)

    @pl.when(k <= 13)
    def _():
        for p in order:
            move(p, lax.rem(k + 2, 16), mv_send.at[p], mv_recv.at[p]).start()
        kinds(2).start()

    @pl.when(k <= 14)
    def _():
        kinds(1).start()

    @pl.when(k == 0)
    def _():
        for p in order:
            move(p, 1, mv_extra.at[p], mv_recv.at[p]).start()
        for p in order:
            pltpu.make_async_copy(inc.at[p], lev.at[OWN + p], mv_recv.at[p]).start()

    field_right(1).start()
    field_left(1).start()

    def arrive(p):
        @pl.when(k == 0)
        def _():
            pltpu.make_async_copy(inc.at[p], lev.at[OWN + p], mv_recv.at[p]).wait()

        @pl.when(k > 0)
        def _():
            move(p, lax.rem(k + 2, 16), mv_send.at[p], mv_recv.at[p]).wait_recv()

    arrive(3)
    halo_right(1).start()
    arrive(0)
    halo_left(1).start()
    arrive(2)
    halo_right(2).start()
    arrive(1)
    halo_left(2).start()
    halo_right(3).start()
    halo_left(3).start()
    halo_right(4).start()
    halo_left(4).start()

    @pl.when(k >= 1)
    def _():
        kinds(1).wait_recv()

    @pl.when(k >= 2)
    def _():
        kinds(2).wait_recv()

    lane = lax.broadcasted_iota(jnp.int32, (ORIENT, 128), 1)
    in_low = lane < 64
    at_first = lax.rem(lane, 64) == 0
    at_last = lax.rem(lane, 64) == 63

    def blend(p, src, kinds_row):
        ax0, ax2, la0, la2, de0, de2 = [taps[n] for n in range(6)]
        halves = []
        for h in range(2):
            lanes = pl.ds(128 * h, 128)
            halves.append(
                ax0 * lev[src + p - 1, :, lanes] + lev[src + p, :, lanes] + ax2 * lev[src + p + 1, :, lanes]
            )
        a0, a1 = halves
        r0 = pltpu.roll(a0, 64, 1)
        r1 = pltpu.roll(a1, 64, 1)
        near = jnp.where(in_low, r1, r0)
        far = jnp.where(in_low, r0, r1)
        b0 = la0 * near + a0 + la2 * far
        b1 = la0 * far + a1 + la2 * near
        es = []
        for b in (b0, b1):
            turned = pltpu.roll(b, 64, 1)
            behind = pltpu.roll(jnp.where(at_last, turned, b), 1, 1)
            ahead = pltpu.roll(jnp.where(at_first, turned, b), 127, 1)
            es.append(de0 * behind + b + de2 * ahead)
        e = jnp.concatenate(es, axis=1)
        e_high = e.astype(jnp.bfloat16)
        e_low = (e - e_high.astype(jnp.float32)).astype(jnp.bfloat16)
        stacked = jnp.concatenate([e_high, e_high, e_low], axis=0)
        c = jnp.dot(kcat[...], stacked, preferred_element_type=jnp.float32)
        chosen = jnp.where(kinds_row == 0.0, fw[p, 0], jnp.where(kinds_row == 1.0, fw[p, 1], fw[p, 2]))
        return c * jnp.exp(-chosen)

    def stage_steps(d, s, carry):
        row = bt[s - 1]
        restart0 = jnp.logical_and(k == 0, s == 9)
        restart1 = jnp.logical_and(k == 1, s == 5)
        level = jnp.where(jnp.logical_or(restart0, restart1), 0, s - 1)
        src = level * SPAN
        p_left = OWN - d + s
        p_right = OWN + PLANES - 1 + d - s
        new_left = blend(p_left, src, row)
        new_right = blend(p_right, src, row)
        lev[s * SPAN + p_left] = new_left
        lev[s * SPAN + p_right] = new_right
        return carry

    stage_steps(0, 1, 0)

    def stage(d, carry):
        halo_right(d).wait_recv()

        @pl.when(d <= LEVELS - PLANES)
        def _():
            halo_right(d + PLANES).start()

        halo_left(d).wait_recv()

        @pl.when(d <= LEVELS - PLANES)
        def _():
            halo_left(d + PLANES).start()

        @pl.when(lax.rem(d, 4) == 1)
        def _():
            r = lax.div(d + 3, 4)
            field_right(r).wait_recv()
            field_left(r).wait_recv()

            @pl.when(r < 3)
            def _():
                field_right(r + 1).start()
                field_left(r + 1).start()

        lax.fori_loop(1, jnp.minimum(d + 1, LEVELS) + 1, functools.partial(stage_steps, d), 0)
        return carry

    lax.fori_loop(1, LEVELS + 1, stage, 0)

    for p in range(PLANES):
        hand[p] = lev[LEVELS * SPAN + OWN + p]
        for n in range(8):
            rows = pl.ds(8 * n, 8)
            total = jnp.zeros((8, CELLS), jnp.float32)
            for j in range(4):
                total += lev[(9 + j) * SPAN + OWN + p, rows] * back[j, p, rows].astype(jnp.float32)
            part[0, n % 4, n // 4, p] = total[:4]
            part[1, n % 4, n // 4, p] = total[4:]

    to_core = pltpu.make_async_remote_copy(
        src_ref=part.at[1 - core], dst_ref=r_core, send_sem=c_send, recv_sem=c_recv,
        device_id=(other_core, g), device_id_type=MESH,
    )
    to_core.start()
    to_core.wait_recv()
    summed[...] = part[core] + r_core[...]

    def to_y(dy):
        return pltpu.make_async_remote_copy(
            src_ref=summed.at[lax.rem(y + dy, 4)], dst_ref=r_y.at[dy - 1],
            send_sem=y_send.at[dy - 1], recv_sem=y_recv.at[dy - 1],
            device_id=(across(dy), g), device_id_type=MESH,
        )

    for dy in (2, 1, 3):
        to_y(dy).start()
    for dy in (1, 3, 2):
        to_y(dy).wait_recv()
    s_y[...] = summed[y] + r_y[0] + r_y[1] + r_y[2]
    to_z = pltpu.make_async_remote_copy(
        src_ref=s_y.at[1 - zhi], dst_ref=r_z, send_sem=z_send, recv_sem=z_recv,
        device_id=(other_z, g), device_id_type=MESH,
    )
    to_z.start()

    def drain(d, carry):
        halo_right(d).wait_send()
        halo_left(d).wait_send()
        return carry

    lax.fori_loop(1, LEVELS + 1, drain, 0)
    for r in (1, 2, 3):
        field_right(r).wait_send()
        field_left(r).wait_send()

    @pl.when(k <= 13)
    def _():
        for p in order:
            move(p, lax.rem(k + 2, 16), mv_send.at[p], mv_recv.at[p]).wait_send()
        kinds(2).wait_send()

    @pl.when(k <= 14)
    def _():
        kinds(1).wait_send()

    @pl.when(k == 0)
    def _():
        for p in order:
            move(p, 1, mv_extra.at[p], mv_recv.at[p]).wait_send()

    to_core.wait_send()
    for dy in (1, 2, 3):
        to_y(dy).wait_send()
    to_z.wait()
    den[...] = (s_y[zhi] + r_z[...]) / contour


def per_device(
    incoming, backward, fields, block_types,
    axial_taps, lateral_taps, depth_taps, bend_diagonal, bend_coupling,
):
    n_gx = lax.axis_size("gx")
    contour = float(lax.axis_size("sec") * block_types.shape[1])
    ratios = jnp.stack(
        [t[n] / t[1] for t in (axial_taps, lateral_taps, depth_taps) for n in (0, 2)]
    )
    taps = jnp.broadcast_to(ratios[:, :, None], (6, ORIENT, 128))
    kernel = jnp.diag(bend_diagonal) + bend_coupling
    kernel = kernel * (axial_taps[1] * lateral_taps[1] * depth_taps[1])[None, :]
    kmat = jnp.concatenate([kernel, kernel, kernel], axis=1)
    fld = jnp.transpose(fields, (1, 0, 2))[:, :, None, :]
    btr = jnp.broadcast_to(block_types[0].astype(jnp.float32)[:, None, None], (4, 1, CELLS))
    vmem = pl.BlockSpec(memory_space=pltpu.VMEM)
    dma = pltpu.SemaphoreType.DMA
    f32 = jnp.float32
    hand, den = pl.pallas_call(
        functools.partial(body, n_gx, contour),
        out_shape=(
            jax.ShapeDtypeStruct((PLANES, ORIENT, CELLS), f32),
            jax.ShapeDtypeStruct((PLANES, 4, CELLS), f32),
        ),
        in_specs=[vmem] * 6,
        out_specs=(vmem, vmem),
        scratch_shapes=[
            pltpu.VMEM(((LEVELS + 1) * SPAN, ORIENT, CELLS), f32),
            pltpu.VMEM((SPAN, 3, 1, CELLS), f32),
            pltpu.VMEM((LEVELS, 1, CELLS), f32),
            pltpu.VMEM((2, 4, 2, PLANES, 4, CELLS), f32),
            pltpu.VMEM((4, 2, PLANES, 4, CELLS), f32),
            pltpu.VMEM((ORIENT, 3 * ORIENT), jnp.bfloat16),
            pltpu.VMEM((4, 2, PLANES, 4, CELLS), f32),
            pltpu.VMEM((3, 2, PLANES, 4, CELLS), f32),
            pltpu.VMEM((2, PLANES, 4, CELLS), f32),
            pltpu.VMEM((PLANES, 4, CELLS), f32),
            dma((4,)), dma((4,)), dma((4,)),
            dma((2, LEVELS)), dma((2, LEVELS)),
            dma((2, 3)), dma((2, 3)),
            dma((2,)), dma((2,)),
            dma((2,)),
            dma(()), dma(()),
            dma((3,)), dma((3,)),
            dma(()), dma(()),
        ],
        compiler_params=pltpu.CompilerParams(
            collective_id=0, has_side_effects=True, vmem_limit_bytes=48 << 20
        ),
        name="chain",
    )(incoming[0], backward, fld, btr, taps, kmat)
    return hand[None], den


def solution(mesh):
    in_specs = (
        P("sec", "gx", None, None),
        P("sec", "gx", None, None),
        P(None, "gx", None),
        P("sec", None),
        P(), P(), P(), P(), P(),
    )
    out_specs = (P("sec", "gx", None, None), P("gx", "sec", None))
    return jax.shard_map(
        per_device, mesh=mesh, in_specs=in_specs, out_specs=out_specs, check_vma=False
    )
```

time: 553 us -> 117 us (0.21)
  waiting for transfers between devices: 313 us -> 0 us
  starting transfers between devices: 192 us -> 0 us
  Pallas kernels: 0 us -> 110 us
  between operations: 16 us -> 0.7 us
  matrix products: 9.86 us -> 0 us
  local copies, waits for them, and re-layouts: 13.1 us -> 3.28 us
  other arithmetic: 8.28 us -> 2.37 us
    unnamed x2 -> x0, waiting for transfers between devices: 280 us -> none
    ppermute x26 -> x0, starting transfers between devices: 192 us -> none  [the longest x12 150 us: padded_2(): lax.ppermute(lax.slice_in_dim(block, 0, width, axis=dim), axis, backward)]
    pallas_call x0 -> x1, Pallas kernels: none -> 110 us  [per_device(): pl.pallas_call(functools.partial(body, n_gx, contour), out_shape=(jax.Sha...]
    ppermute x26 -> x0, waiting for transfers between devices: 32.3 us -> none  [the longest x12 13 us: padded_2(): lax.ppermute(lax.slice_in_dim(block, 0, width, axis=dim), axis, backward)]
    dot_general x12 -> x0, matrix products: 9.86 us -> none  [advance_padded(): jnp.einsum('uv,xvc->xuc', kernel, along_z, precision=lax.Precision.HIGHES...]
    slice x85 -> x0, local copies, waits for them, and re-layouts: 9.85 us -> none  [the longest x24 2.75 us: advance_padded(): jnp.roll(along_y, CZ - 1, axis=2)]
  transfers between devices with their start and end apart: 27 -> 0, of which waited for: 15 -> 0; matrix products, arithmetic and copies ran while one was open for 1% -> 0% of each run, Pallas kernels for 0% -> 0%
where the time goes in v1:
time: 117 us; the launch traced here: 116 us
  Pallas kernels  110 us (94%)
  local copies, waits for them, and re-layouts  3.28 us (3%)
  other arithmetic  2.37 us (2%)
    pallas_call x1, Pallas kernels, per_device(): pl.pallas_call(functools.partial(body, n_gx, contour), out_shape=(jax.Sha...  110 us
    unnamed x8, local copies, waits for them, and re-layouts  2.36 us

profile of v1, /device:TPU:1, one launch (start us, length us, event | category | flops | bytes accessed | tf_op | source)
XLA Modules:
  0.0 115.9 jit_solution(18338778517059889579)
XLA Ops:
  0.6 0.0 copy-start.2
  0.6 0.0 copy-start.1
  0.6 0.7 convert_bitcast_fusion
  1.4 0.1 broadcast_in_dim.38.btr
  1.4 0.8 multiply_bitcast_fusion
  2.3 0.7 copy.12.fld
  3.0 0.0 copy-done.2
  3.0 0.7 add_multiply_fusion
  3.8 0.1 pad_maximum_fusion.kmat
  3.9 0.1 broadcast_in_dim.39.taps
  4.0 0.0 copy-done.1
  4.0 0.0 copy-start
  4.0 1.0 copy-done
  5.0 109.6 %chain.1 = (f32[4,64,256]{2,1,0:T(8,128)S(1)}, f32[4,4,256]{2,1,0:T(4,128)S(1)}) custom-call(f32[4,64,256]{2,1,0:T(8,128)S(1)} %bitcast.10, bf16[4,4,64,256]{3,2,1,0:T(8,128)(2,1)S(1)} %copy-done, f32[4,3,1,256]{3,2,1,0:T(1,128)S(1)} %copy.12.fld, f32[4,1,256]{2,1,0:T(1,128)S(1)} %broadcast_in_dim.38.btr, f32[6,64,128]{2,1,0:T(8,128)S(1)} %broadcast_in_dim.39.taps, ...), custom_call_target="tpu_custom_call" | custom-call | tf_op jit(solution)/shard_map/chain/pallas_call | solution.py:326
  114.6 0.7 copy.15
  115.3 0.6 copy.16
  (1 shorter events, 0.0 us)
Async XLA Ops:
  0.6 2.4 %copy-start.2 = (f32[64,64]{1,0:T(8,128)S(1)}, f32[64,64]{1,0:T(8,128)}, u32[]{:S(2)}) copy-start(f32[64,64]{1,0:T(8,128)} %param.17) | copy-start | bytes 49156
  0.6 3.3 %copy-start.1 = (f32[1,4,64,256]{3,2,1,0:T(8,128)S(1)}, f32[1,4,64,256]{3,2,1,0:T(8,128)}, u32[]{:S(2)}) copy-start(f32[1,4,64,256]{3,2,1,0:T(8,128)} %param.9) | copy-start | bytes 786436
  4.0 1.0 copy-start

commit v2 on v1

--- a/solution.py
+++ b/solution.py
@@ -14,14 +14,15 @@
 OWN = LEVELS
 ORIENT = 64
 CELLS = 256
+SLOTS = 15
 
 
 def body(
     n_gx, contour,
-    inc, back, fld, btr, taps, kmat,
+    inc, back, fld, btr, taps, weights,
     hand, den,
-    lev, fw, bt, part, summed, kcat, r_core, r_y, s_y, r_z,
-    mv_send, mv_recv, mv_extra, h_send, h_recv, f_send, f_recv, b_send, b_recv,
+    lev, q, pad, fw, factors, bt, pick, back_t, wcat, part, summed, relay, r_core, r_y, s_y, r_z,
+    mv_send, mv_recv, mv_extra, relay_sem, h_send, h_recv, f_send, f_recv, b_send, b_recv,
     loc, c_send, c_recv, y_send, y_recv, z_send, z_recv,
 ):
     k = lax.axis_index("sec")
@@ -33,11 +34,13 @@
     left = lax.rem(g + n_gx - 1, n_gx)
     other_core = k + 1 - 2 * core
     other_z = lax.rem(k + 8, 16)
+    relays = k < 6
+    crosses = jnp.logical_and(k >= 6, k <= 7)
 
     def across(dy):
         return 8 * zhi + 2 * lax.rem(y + dy, 4) + core
 
-    bt[pl.ds(0, 8)] = jnp.zeros((8, 1, CELLS), jnp.float32)
+    bt[pl.ds(0, 8)] = jnp.zeros((8, 1, 128), jnp.float32)
     barrier = pltpu.get_barrier_semaphore()
     sections = [lax.rem(k + n, 16) for n in (1, 2, 14, 15)]
     sections += [other_core, other_z] + [across(n) for n in (1, 2, 3)]
@@ -46,27 +49,67 @@
     for n in (left, right):
         pl.semaphore_signal(barrier, inc=1, device_id=(k, n), device_id_type=MESH)
 
-    own_fw = pltpu.make_async_copy(fld, fw.at[pl.ds(OWN, PLANES)], loc.at[0])
+    @pl.when(jnp.logical_and(k >= 8, k <= 9))
+    def _():
+        for n in (4, 6):
+            pl.semaphore_signal(barrier, inc=1, device_id=(k - n, g), device_id_type=MESH)
+
+    own_fw = pltpu.make_async_copy(fld, fw.at[3], loc.at[0])
     own_bt = pltpu.make_async_copy(btr, bt.at[pl.ds(8, 4)], loc.at[1])
     own_fw.start()
     own_bt.start()
-    full = kmat[...]
+    full = weights[...]
     high = full.astype(jnp.bfloat16)
     low = (full - high.astype(jnp.float32)).astype(jnp.bfloat16)
-    col = lax.broadcasted_iota(jnp.int32, full.shape, 1)
-    mixed = jnp.where(
-        jnp.logical_and(col >= ORIENT, col < 2 * ORIENT), low.astype(jnp.float32), high.astype(jnp.float32)
-    )
-    kcat[...] = mixed.astype(jnp.bfloat16)
+    for n in range(2):
+        wcat[pl.ds(128 * n, 128), pl.ds(0, 128)] = high
+        wcat[pl.ds(128 * n, 128), pl.ds(128, 128)] = low
+    for j in range(4):
+        for n, (p_left, p_right) in enumerate(((1, 2), (0, 3))):
+            both = jnp.concatenate([back[j, p_left], back[j, p_right]], axis=0)
+            back_t[j, n] = jnp.transpose(both.astype(jnp.float32))
     own_fw.wait()
     own_bt.wait()
 
-    pl.semaphore_wait(barrier, 11)
+    def pair_factor(j, slab_left, row_left, slab_right, row_right):
+        rows = []
+        for t in range(3):
+            rows.append(jnp.exp(-fw[slab_left, t, pl.ds(row_left, 1)]))
+            rows.append(jnp.exp(-fw[slab_right, t, pl.ds(row_right, 1)]))
+        rows = jnp.concatenate(rows + [jnp.zeros((2, CELLS), jnp.float32)], axis=0)
+        first = rows.astype(jnp.bfloat16).astype(jnp.float32)
+        rest = rows - first
+        second = rest.astype(jnp.bfloat16).astype(jnp.float32)
+        stack = [first, second, rest - second, jnp.zeros((104, CELLS), jnp.float32)]
+        factors[j] = jnp.transpose(jnp.concatenate(stack, axis=0)).astype(jnp.bfloat16)
+
+    pair_factor(0, 3, 1, 3, 2)
+    pair_factor(1, 3, 0, 3, 3)
+
+    @pl.when(jnp.logical_and(k >= 2, k <= 5))
+    def _():
+        pl.semaphore_wait(barrier, 12)
+
+    @pl.when(jnp.logical_or(k < 2, k > 5))
+    def _():
+        pl.semaphore_wait(barrier, 11)
 
     def move(p, target, send, recv):
         return pltpu.make_async_remote_copy(
             src_ref=inc.at[p], dst_ref=lev.at[OWN + p], send_sem=send, recv_sem=recv,
             device_id=(target, g), device_id_type=MESH,
+        )
+
+    def to_relay(p):
+        return pltpu.make_async_remote_copy(
+            src_ref=inc.at[p], dst_ref=relay, send_sem=mv_send.at[p], recv_sem=relay_sem.at[0],
+            device_id=(2 * p + core, g), device_id_type=MESH,
+        )
+
+    def from_relay():
+        return pltpu.make_async_remote_copy(
+            src_ref=relay, dst_ref=lev.at[OWN + y], send_sem=relay_sem.at[1], recv_sem=mv_recv.at[y],
+            device_id=(8 + core, g), device_id_type=MESH,
         )
 
     def halo_right(d):
@@ -85,16 +128,14 @@
 
     def field_right(r):
         return pltpu.make_async_remote_copy(
-            src_ref=fw.at[pl.ds(OWN + PLANES - PLANES * r, PLANES)],
-            dst_ref=fw.at[pl.ds(OWN - PLANES * r, PLANES)],
+            src_ref=fw.at[4 - r], dst_ref=fw.at[3 - r],
             send_sem=f_send.at[0, r - 1], recv_sem=f_recv.at[0, r - 1],
             device_id=(k, right), device_id_type=MESH,
         )
 
     def field_left(r):
         return pltpu.make_async_remote_copy(
-            src_ref=fw.at[pl.ds(OWN - PLANES + PLANES * r, PLANES)],
-            dst_ref=fw.at[pl.ds(OWN + PLANES * r, PLANES)],
+            src_ref=fw.at[2 + r], dst_ref=fw.at[3 + r],
             send_sem=f_send.at[1, r - 1], recv_sem=f_recv.at[1, r - 1],
             device_id=(k, left), device_id_type=MESH,
         )
@@ -107,11 +148,21 @@
         )
 
     order = (3, 0, 2, 1)
-
-    @pl.when(k <= 13)
+    plain_move = jnp.logical_and(k <= 13, jnp.logical_not(crosses))
+
+    @pl.when(crosses)
+    def _():
+        move(3, lax.rem(k + 2, 16), mv_send.at[3], mv_recv.at[3]).start()
+        for p in (0, 2, 1):
+            to_relay(p).start()
+
+    @pl.when(plain_move)
     def _():
         for p in order:
             move(p, lax.rem(k + 2, 16), mv_send.at[p], mv_recv.at[p]).start()
+
+    @pl.when(k <= 13)
+    def _():
         kinds(2).start()
 
     @pl.when(k <= 14)
@@ -127,6 +178,11 @@
 
     field_right(1).start()
     field_left(1).start()
+
+    @pl.when(relays)
+    def _():
+        to_relay(0).wait_recv()
+        from_relay().start()
 
     def arrive(p):
         @pl.when(k == 0)
@@ -158,52 +214,56 @@
     def _():
         kinds(2).wait_recv()
 
-    lane = lax.broadcasted_iota(jnp.int32, (ORIENT, 128), 1)
-    in_low = lane < 64
-    at_first = lax.rem(lane, 64) == 0
-    at_last = lax.rem(lane, 64) == 63
-
-    def blend(p, src, kinds_row):
-        ax0, ax2, la0, la2, de0, de2 = [taps[n] for n in range(6)]
-        halves = []
-        for h in range(2):
-            lanes = pl.ds(128 * h, 128)
-            halves.append(
-                ax0 * lev[src + p - 1, :, lanes] + lev[src + p, :, lanes] + ax2 * lev[src + p + 1, :, lanes]
-            )
-        a0, a1 = halves
-        r0 = pltpu.roll(a0, 64, 1)
-        r1 = pltpu.roll(a1, 64, 1)
-        near = jnp.where(in_low, r1, r0)
-        far = jnp.where(in_low, r0, r1)
-        b0 = la0 * near + a0 + la2 * far
-        b1 = la0 * far + a1 + la2 * near
-        es = []
-        for b in (b0, b1):
-            turned = pltpu.roll(b, 64, 1)
-            behind = pltpu.roll(jnp.where(at_last, turned, b), 1, 1)
-            ahead = pltpu.roll(jnp.where(at_first, turned, b), 127, 1)
-            es.append(de0 * behind + b + de2 * ahead)
-        e = jnp.concatenate(es, axis=1)
-        e_high = e.astype(jnp.bfloat16)
-        e_low = (e - e_high.astype(jnp.float32)).astype(jnp.bfloat16)
-        stacked = jnp.concatenate([e_high, e_high, e_low], axis=0)
-        c = jnp.dot(kcat[...], stacked, preferred_element_type=jnp.float32)
-        chosen = jnp.where(kinds_row == 0.0, fw[p, 0], jnp.where(kinds_row == 1.0, fw[p, 1], fw[p, 2]))
-        return c * jnp.exp(-chosen)
+    row = lax.broadcasted_iota(jnp.int32, (128, 128), 0)
+    lane = lax.broadcasted_iota(jnp.int32, (128, 128), 1)
+    same_side = lax.rem(row, 2) == lax.div(lane, 64)
+    in_use = jnp.logical_and(row < 24, same_side)
+    kind_of = lax.div(lax.rem(row, 8), 2).astype(jnp.float32)
+
+    def choose(s, carry):
+        hit = jnp.logical_and(in_use, kind_of == bt[s])
+        pick[s] = jnp.where(hit, 1.0, 0.0).astype(jnp.bfloat16)
+        return carry
+
+    lax.fori_loop(0, LEVELS, choose, 0)
+
+    def load_pair(j, p_left, p_right):
+        q[1 + j] = jnp.transpose(jnp.concatenate([lev[p_left], lev[p_right]], axis=0))
+
+    load_pair(0, OWN + 1, OWN + 2)
+    load_pair(1, OWN, OWN + 3)
+    q[0] = pltpu.roll(q[1], 64, 1)
 
     def stage_steps(d, s, carry):
-        row = bt[s - 1]
         restart0 = jnp.logical_and(k == 0, s == 9)
         restart1 = jnp.logical_and(k == 1, s == 5)
         level = jnp.where(jnp.logical_or(restart0, restart1), 0, s - 1)
-        src = level * SPAN
-        p_left = OWN - d + s
-        p_right = OWN + PLANES - 1 + d - s
-        new_left = blend(p_left, src, row)
-        new_right = blend(p_right, src, row)
-        lev[s * SPAN + p_left] = new_left
-        lev[s * SPAN + p_right] = new_right
+        j = 1 + d - s
+        base = level * SLOTS + j
+        ax_out, ax_in, la0, la2, de0, de2 = [taps[pl.ds(n, 1)] for n in range(6)]
+        along_x = []
+        for n in range(4):
+            rows = pl.ds(64 * n, 64)
+            along_x.append(ax_out * q[base + 2, rows] + q[base + 1, rows] + ax_in * q[base, rows])
+        parts = []
+        for n in range(4):
+            b = la0 * along_x[n - 1] + along_x[n] + la2 * along_x[(n + 1) % 4]
+            pad[n, pl.ds(8, 64)] = b
+            pad[n, pl.ds(7, 1)] = b[63:]
+            pad[n, pl.ds(72, 1)] = b[:1]
+            e = de0 * pad[n, pl.ds(7, 64)] + b + de2 * pad[n, pl.ds(9, 64)]
+            e_high = e.astype(jnp.bfloat16)
+            e_low = (e - e_high.astype(jnp.float32)).astype(jnp.bfloat16)
+            parts.append(jnp.concatenate([e_high, e_low], axis=1))
+        c = jnp.dot(jnp.concatenate(parts, axis=0), wcat[...], preferred_element_type=jnp.float32)
+        factor = jnp.dot(factors[j], pick[s - 1], preferred_element_type=jnp.float32)
+        fresh = (c[:, :128] + c[:, 128:]) * factor
+        q[s * SLOTS + j + 1] = fresh
+
+        @pl.when(j == 0)
+        def _():
+            q[s * SLOTS] = pltpu.roll(fresh, 64, 1)
+
         return carry
 
     stage_steps(0, 1, 0)
@@ -232,26 +292,35 @@
                 field_right(r + 1).start()
                 field_left(r + 1).start()
 
+            for n in range(4):
+                pair_factor(1 + d + n, 3 - r, 3 - n, 3 + r, n)
+
+        load_pair(1 + d, OWN - d, OWN + PLANES - 1 + d)
         lax.fori_loop(1, jnp.minimum(d + 1, LEVELS) + 1, functools.partial(stage_steps, d), 0)
         return carry
 
     lax.fori_loop(1, LEVELS + 1, stage, 0)
 
-    for p in range(PLANES):
-        hand[p] = lev[LEVELS * SPAN + OWN + p]
-        for n in range(8):
-            rows = pl.ds(8 * n, 8)
-            total = jnp.zeros((8, CELLS), jnp.float32)
-            for j in range(4):
-                total += lev[(9 + j) * SPAN + OWN + p, rows] * back[j, p, rows].astype(jnp.float32)
-            part[0, n % 4, n // 4, p] = total[:4]
-            part[1, n % 4, n // 4, p] = total[4:]
+    for n, owned in enumerate(((1, 2), (0, 3))):
+        total = q[9 * SLOTS + 1 + n] * back_t[0, n]
+        for j in range(1, 4):
+            total += q[(9 + j) * SLOTS + 1 + n] * back_t[j, n]
+        total = jnp.transpose(total)
+        for side, p in enumerate(owned):
+            for m in range(8):
+                at = 64 * side + 8 * m
+                part[0, m % 4, m // 4, p] = total[at:at + 4]
+                part[1, m % 4, m // 4, p] = total[at + 4:at + 8]
 
     to_core = pltpu.make_async_remote_copy(
         src_ref=part.at[1 - core], dst_ref=r_core, send_sem=c_send, recv_sem=c_recv,
         device_id=(other_core, g), device_id_type=MESH,
     )
     to_core.start()
+    for n, owned in enumerate(((1, 2), (0, 3))):
+        planes = jnp.transpose(q[LEVELS * SLOTS + 1 + n])
+        hand[owned[0]] = planes[:64]
+        hand[owned[1]] = planes[64:]
     to_core.wait_recv()
     summed[...] = part[core] + r_core[...]
 
@@ -298,6 +367,10 @@
         for p in order:
             move(p, 1, mv_extra.at[p], mv_recv.at[p]).wait_send()
 
+    @pl.when(relays)
+    def _():
+        from_relay().wait_send()
+
     to_core.wait_send()
     for dy in (1, 2, 3):
         to_y(dy).wait_send()
@@ -311,15 +384,15 @@
 ):
     n_gx = lax.axis_size("gx")
     contour = float(lax.axis_size("sec") * block_types.shape[1])
-    ratios = jnp.stack(
-        [t[n] / t[1] for t in (axial_taps, lateral_taps, depth_taps) for n in (0, 2)]
+    ax, la, de = axial_taps / axial_taps[1], lateral_taps / lateral_taps[1], depth_taps / depth_taps[1]
+    sides = [(ax[0], ax[2]), (ax[2], ax[0]), (la[0], la[0]), (la[2], la[2]), (de[0], de[0]), (de[2], de[2])]
+    taps = jnp.stack([jnp.concatenate(pair) for pair in sides])
+    kernel = jnp.diag(bend_diagonal) + bend_coupling
+    turned = (kernel * (axial_taps[1] * lateral_taps[1] * depth_taps[1])[None, :]).T
+    weights = jnp.concatenate(
+        [jnp.pad(turned, ((0, 0), (0, ORIENT))), jnp.pad(turned, ((0, 0), (ORIENT, 0)))], axis=0
     )
-    taps = jnp.broadcast_to(ratios[:, :, None], (6, ORIENT, 128))
-    kernel = jnp.diag(bend_diagonal) + bend_coupling
-    kernel = kernel * (axial_taps[1] * lateral_taps[1] * depth_taps[1])[None, :]
-    kmat = jnp.concatenate([kernel, kernel, kernel], axis=1)
-    fld = jnp.transpose(fields, (1, 0, 2))[:, :, None, :]
-    btr = jnp.broadcast_to(block_types[0].astype(jnp.float32)[:, None, None], (4, 1, CELLS))
+    btr = jnp.broadcast_to(block_types[0].astype(jnp.float32)[:, None, None], (4, 1, 128))
     vmem = pl.BlockSpec(memory_space=pltpu.VMEM)
     dma = pltpu.SemaphoreType.DMA
     f32 = jnp.float32
@@ -332,17 +405,23 @@
         in_specs=[vmem] * 6,
         out_specs=(vmem, vmem),
         scratch_shapes=[
-            pltpu.VMEM(((LEVELS + 1) * SPAN, ORIENT, CELLS), f32),
-            pltpu.VMEM((SPAN, 3, 1, CELLS), f32),
-            pltpu.VMEM((LEVELS, 1, CELLS), f32),
+            pltpu.VMEM((SPAN, ORIENT, CELLS), f32),
+            pltpu.VMEM(((LEVELS + 1) * SLOTS, CELLS, 128), f32),
+            pltpu.VMEM((4, 80, 128), f32),
+            pltpu.VMEM((7, 3, PLANES, CELLS), f32),
+            pltpu.VMEM((SLOTS, CELLS, 128), jnp.bfloat16),
+            pltpu.VMEM((LEVELS, 1, 128), f32),
+            pltpu.VMEM((LEVELS, 128, 128), jnp.bfloat16),
+            pltpu.VMEM((4, 2, CELLS, 128), f32),
+            pltpu.VMEM((256, 256), jnp.bfloat16),
             pltpu.VMEM((2, 4, 2, PLANES, 4, CELLS), f32),
             pltpu.VMEM((4, 2, PLANES, 4, CELLS), f32),
-            pltpu.VMEM((ORIENT, 3 * ORIENT), jnp.bfloat16),
+            pltpu.VMEM((ORIENT, CELLS), f32),
             pltpu.VMEM((4, 2, PLANES, 4, CELLS), f32),
             pltpu.VMEM((3, 2, PLANES, 4, CELLS), f32),
             pltpu.VMEM((2, PLANES, 4, CELLS), f32),
             pltpu.VMEM((PLANES, 4, CELLS), f32),
-            dma((4,)), dma((4,)), dma((4,)),
+            dma((4,)), dma((4,)), dma((4,)), dma((2,)),
             dma((2, LEVELS)), dma((2, LEVELS)),
             dma((2, 3)), dma((2, 3)),
             dma((2,)), dma((2,)),
@@ -352,10 +431,10 @@
             dma(()), dma(()),
         ],
         compiler_params=pltpu.CompilerParams(
-            collective_id=0, has_side_effects=True, vmem_limit_bytes=48 << 20
+            collective_id=0, has_side_effects=True, vmem_limit_bytes=52 << 20
         ),
         name="chain",
-    )(incoming[0], backward, fld, btr, taps, kmat)
+    )(incoming[0], backward, fields, btr, taps, weights)
     return hand[None], den
 
 

time: 117 us -> 93.3 us (0.80)
  the two profiles are of different devices: /device:TPU:1 before, /device:TPU:9 now
where the time goes in v2:
time: 93.3 us; the launch traced here: 92.9 us
  Pallas kernels  84.3 us (90%)
  local copies, waits for them, and re-layouts  4.57 us (5%)
  other arithmetic  3.32 us (4%)
    pallas_call x1, Pallas kernels, per_device(): pl.pallas_call(functools.partial(body, n_gx, contour), out_shape=(jax.Sha...  84.3 us
    unnamed x11, local copies, waits for them, and re-layouts  4.46 us

profile of v2, /device:TPU:9, one launch (start us, length us, event | category | flops | bytes accessed | tf_op | source)
XLA Modules:
  0.0 92.9 jit_solution(5315299761999424947)
XLA Ops:
  0.6 0.0 copy-start.3
  0.6 0.0 copy-start.1
  0.6 0.6 copy-done.3
  1.3 0.1 broadcast_in_dim.28.btr
  1.4 0.7 multiply_bitcast_fusion.1
  2.1 0.7 broadcast_divide_fusion.2
  2.8 0.1 maximum_bitcast_fusion.1
  2.9 0.7 broadcast_divide_fusion
  3.6 0.1 maximum_bitcast_fusion.5
  3.6 0.1 maximum_bitcast_fusion.4
  3.7 0.1 maximum_bitcast_fusion.3
  3.8 0.1 maximum_bitcast_fusion.2
  3.9 0.8 copy.11
  4.7 0.7 multiply_bitcast_fusion
  5.5 0.0 copy-start.2
  5.5 0.1 select_maximum_fusion.weights
  5.6 0.0 copy-done.1
  5.6 0.6 copy-done.2
  6.2 0.0 copy-start
  6.2 1.0 %copy-done = bf16[4,4,64,256]{3,2,1,0:T(8,128)(2,1)S(1)} copy-done((bf16[4,4,64,256]{3,2,1,0:T(8,128)(2,1)S(1)}, bf16[4,4,64,256]{3,2,1,0:T(8,128)(2,1)}, u32[]{:S(2)}) %copy-start) | copy-done | bytes 524312
  7.2 84.3 %chain.1 = (f32[4,64,256]{2,1,0:T(8,128)S(1)}, f32[4,4,256]{2,1,0:T(4,128)S(1)}) custom-call(f32[4,64,256]{2,1,0:T(8,128)S(1)} %bitcast.38, bf16[4,4,64,256]{3,2,1,0:T(8,128)(2,1)S(1)} %copy-done, f32[3,4,256]{2,1,0:T(4,128)S(1)} %copy-done.2, f32[4,1,128]{2,1,0:T(1,128)S(1)} %broadcast_in_dim.28.btr, f32[6,128]{1,0:T(8,128)S(1)} %stack.27.taps, ...), custom_call_target="tpu_custom_call" | custom-call | tf_op jit(solution)/shard_map/chain/pallas_call | solution.py:399
  91.6 0.7 copy.14
  92.3 0.6 copy.15
  (5 shorter events, 0.0 us)
Async XLA Ops:
  0.6 0.7 copy-start.3
  0.6 4.9 %copy-start.1 = (f32[1,4,64,256]{3,2,1,0:T(8,128)S(1)}, f32[1,4,64,256]{3,2,1,0:T(8,128)}, u32[]{:S(2)}) copy-start(f32[1,4,64,256]{3,2,1,0:T(8,128)} %param.9) | copy-start | bytes 786436
  5.5 0.7 copy-start.2
  6.2 1.0 %copy-start = (bf16[4,4,64,256]{3,2,1,0:T(8,128)(2,1)S(1)}, bf16[4,4,64,256]{3,2,1,0:T(8,128)(2,1)}, u32[]{:S(2)}) copy-start(bf16[4,4,64,256]{3,2,1,0:T(8,128)(2,1)} %back.1) | copy-start | bytes 1572868

commit v3 on v2

--- a/solution.py
+++ b/solution.py
@@ -19,9 +19,10 @@
 
 def body(
     n_gx, contour,
-    inc, back, fld, btr, taps, weights,
+    inc_hbm, back, fld, btr_hbm, ax_hbm, la_hbm, de_hbm, diagonal_hbm, coupling_hbm,
     hand, den,
-    lev, q, pad, fw, factors, bt, pick, back_t, wcat, part, summed, relay, r_core, r_y, s_y, r_z,
+    inc, btr, ax_taps, la_taps, de_taps, diagonal, coupling,
+    lev, q, pad, fw, factors, bt, pick, scaled, held, back_t, wcat, taps, part, summed, relay, r_core, r_y, s_y, r_z,
     mv_send, mv_recv, mv_extra, relay_sem, h_send, h_recv, f_send, f_recv, b_send, b_recv,
     loc, c_send, c_recv, y_send, y_recv, z_send, z_recv,
 ):
@@ -40,7 +41,16 @@
     def across(dy):
         return 8 * zhi + 2 * lax.rem(y + dy, 4) + core
 
-    bt[pl.ds(0, 8)] = jnp.zeros((8, 1, 128), jnp.float32)
+    fetches = [
+        pltpu.make_async_copy(src, dst, loc.at[n])
+        for n, (src, dst) in enumerate((
+            (inc_hbm.at[0], inc), (btr_hbm, btr), (fld, fw.at[3]), (ax_hbm, ax_taps), (la_hbm, la_taps),
+            (de_hbm, de_taps), (diagonal_hbm, diagonal), (coupling_hbm, coupling), (back, held),
+        ))
+    ]
+    for fetch in fetches:
+        fetch.start()
+    bt[...] = jnp.zeros((3, 1, 4), jnp.int32)
     barrier = pltpu.get_barrier_semaphore()
     sections = [lax.rem(k + n, 16) for n in (1, 2, 14, 15)]
     sections += [other_core, other_z] + [across(n) for n in (1, 2, 3)]
@@ -54,23 +64,30 @@
         for n in (4, 6):
             pl.semaphore_signal(barrier, inc=1, device_id=(k - n, g), device_id_type=MESH)
 
-    own_fw = pltpu.make_async_copy(fld, fw.at[3], loc.at[0])
-    own_bt = pltpu.make_async_copy(btr, bt.at[pl.ds(8, 4)], loc.at[1])
-    own_fw.start()
-    own_bt.start()
-    full = weights[...]
+    for fetch in fetches[:-1]:
+        fetch.wait()
+    ax, la, de = [t[...] for t in (ax_taps, la_taps, de_taps)]
+
+    def lanes(t, n, m):
+        return jnp.concatenate([t[n:n + 1] / t[1:2], t[m:m + 1] / t[1:2]], axis=1)
+
+    for n, one in enumerate(
+        (lanes(ax, 0, 2), lanes(ax, 2, 0), lanes(la, 0, 0), lanes(la, 2, 2), lanes(de, 0, 0), lanes(de, 2, 2))
+    ):
+        taps[pl.ds(n, 1)] = one
+    square = (ORIENT, ORIENT)
+    on_diagonal = lax.broadcasted_iota(jnp.int32, square, 0) == lax.broadcasted_iota(jnp.int32, square, 1)
+    kernel = coupling[...] + jnp.where(on_diagonal, jnp.broadcast_to(diagonal[...], square), 0.0)
+    turned = jnp.transpose(kernel * (ax[1:2] * la[1:2] * de[1:2]))
+    none = jnp.zeros(square, jnp.float32)
+    full = jnp.concatenate(
+        [jnp.concatenate([turned, none], axis=1), jnp.concatenate([none, turned], axis=1)], axis=0
+    )
     high = full.astype(jnp.bfloat16)
     low = (full - high.astype(jnp.float32)).astype(jnp.bfloat16)
     for n in range(2):
         wcat[pl.ds(128 * n, 128), pl.ds(0, 128)] = high
         wcat[pl.ds(128 * n, 128), pl.ds(128, 128)] = low
-    for j in range(4):
-        for n, (p_left, p_right) in enumerate(((1, 2), (0, 3))):
-            both = jnp.concatenate([back[j, p_left], back[j, p_right]], axis=0)
-            back_t[j, n] = jnp.transpose(both.astype(jnp.float32))
-    own_fw.wait()
-    own_bt.wait()
-
     def pair_factor(j, slab_left, row_left, slab_right, row_right):
         rows = []
         for t in range(3):
@@ -142,7 +159,7 @@
 
     def kinds(ahead):
         return pltpu.make_async_remote_copy(
-            src_ref=btr, dst_ref=bt.at[pl.ds(8 - 4 * ahead, 4)],
+            src_ref=btr, dst_ref=bt.at[2 - ahead],
             send_sem=b_send.at[ahead - 1], recv_sem=b_recv.at[ahead - 1],
             device_id=(lax.rem(k + ahead, 16), g), device_id_type=MESH,
         )
@@ -178,6 +195,12 @@
 
     field_right(1).start()
     field_left(1).start()
+
+    fetches[-1].wait()
+    for j in range(4):
+        for n, (p_left, p_right) in enumerate(((1, 2), (0, 3))):
+            both = jnp.concatenate([held[j, p_left], held[j, p_right]], axis=0)
+            back_t[j, n] = jnp.transpose(both.astype(jnp.float32))
 
     @pl.when(relays)
     def _():
@@ -201,10 +224,9 @@
     halo_right(2).start()
     arrive(1)
     halo_left(2).start()
-    halo_right(3).start()
-    halo_left(3).start()
-    halo_right(4).start()
-    halo_left(4).start()
+    for d in (3, 4):
+        halo_right(d).start()
+        halo_left(d).start()
 
     @pl.when(k >= 1)
     def _():
@@ -218,14 +240,14 @@
     lane = lax.broadcasted_iota(jnp.int32, (128, 128), 1)
     same_side = lax.rem(row, 2) == lax.div(lane, 64)
     in_use = jnp.logical_and(row < 24, same_side)
-    kind_of = lax.div(lax.rem(row, 8), 2).astype(jnp.float32)
-
-    def choose(s, carry):
-        hit = jnp.logical_and(in_use, kind_of == bt[s])
+    kind_of = lax.div(lax.rem(row, 8), 2)
+    step_of = lax.broadcasted_iota(jnp.int32, (1, 4), 1)
+
+    for s in range(LEVELS):
+        own = btr[...] if s >= 8 else bt[s // 4]
+        kind = jnp.sum(jnp.where(step_of == s % 4, own, 0), axis=1, keepdims=True)
+        hit = jnp.logical_and(in_use, kind_of == jnp.broadcast_to(kind, (128, 128)))
         pick[s] = jnp.where(hit, 1.0, 0.0).astype(jnp.bfloat16)
-        return carry
-
-    lax.fori_loop(0, LEVELS, choose, 0)
 
     def load_pair(j, p_left, p_right):
         q[1 + j] = jnp.transpose(jnp.concatenate([lev[p_left], lev[p_right]], axis=0))
@@ -241,6 +263,7 @@
         j = 1 + d - s
         base = level * SLOTS + j
         ax_out, ax_in, la0, la2, de0, de2 = [taps[pl.ds(n, 1)] for n in range(6)]
+        scaled[...] = jnp.dot(factors[j], pick[s - 1], preferred_element_type=jnp.float32)
         along_x = []
         for n in range(4):
             rows = pl.ds(64 * n, 64)
@@ -256,13 +279,12 @@
             e_low = (e - e_high.astype(jnp.float32)).astype(jnp.bfloat16)
             parts.append(jnp.concatenate([e_high, e_low], axis=1))
         c = jnp.dot(jnp.concatenate(parts, axis=0), wcat[...], preferred_element_type=jnp.float32)
-        factor = jnp.dot(factors[j], pick[s - 1], preferred_element_type=jnp.float32)
-        fresh = (c[:, :128] + c[:, 128:]) * factor
+        fresh = (c[:, :128] + c[:, 128:]) * scaled[...]
         q[s * SLOTS + j + 1] = fresh
 
         @pl.when(j == 0)
         def _():
-            q[s * SLOTS] = pltpu.roll(fresh, 64, 1)
+            q[s * SLOTS] = pltpu.roll(q[s * SLOTS + 1], 64, 1)
 
         return carry
 
@@ -384,16 +406,8 @@
 ):
     n_gx = lax.axis_size("gx")
     contour = float(lax.axis_size("sec") * block_types.shape[1])
-    ax, la, de = axial_taps / axial_taps[1], lateral_taps / lateral_taps[1], depth_taps / depth_taps[1]
-    sides = [(ax[0], ax[2]), (ax[2], ax[0]), (la[0], la[0]), (la[2], la[2]), (de[0], de[0]), (de[2], de[2])]
-    taps = jnp.stack([jnp.concatenate(pair) for pair in sides])
-    kernel = jnp.diag(bend_diagonal) + bend_coupling
-    turned = (kernel * (axial_taps[1] * lateral_taps[1] * depth_taps[1])[None, :]).T
-    weights = jnp.concatenate(
-        [jnp.pad(turned, ((0, 0), (0, ORIENT))), jnp.pad(turned, ((0, 0), (ORIENT, 0)))], axis=0
-    )
-    btr = jnp.broadcast_to(block_types[0].astype(jnp.float32)[:, None, None], (4, 1, 128))
     vmem = pl.BlockSpec(memory_space=pltpu.VMEM)
+    hbm = pl.BlockSpec(memory_space=pltpu.HBM)
     dma = pltpu.SemaphoreType.DMA
     f32 = jnp.float32
     hand, den = pl.pallas_call(
@@ -402,18 +416,28 @@
             jax.ShapeDtypeStruct((PLANES, ORIENT, CELLS), f32),
             jax.ShapeDtypeStruct((PLANES, 4, CELLS), f32),
         ),
-        in_specs=[vmem] * 6,
+        in_specs=[hbm] * 9,
         out_specs=(vmem, vmem),
         scratch_shapes=[
+            pltpu.VMEM((PLANES, ORIENT, CELLS), f32),
+            pltpu.VMEM((1, 4), jnp.int32),
+            pltpu.VMEM((3, ORIENT), f32),
+            pltpu.VMEM((3, ORIENT), f32),
+            pltpu.VMEM((3, ORIENT), f32),
+            pltpu.VMEM((1, ORIENT), f32),
+            pltpu.VMEM((ORIENT, ORIENT), f32),
             pltpu.VMEM((SPAN, ORIENT, CELLS), f32),
             pltpu.VMEM(((LEVELS + 1) * SLOTS, CELLS, 128), f32),
             pltpu.VMEM((4, 80, 128), f32),
             pltpu.VMEM((7, 3, PLANES, CELLS), f32),
             pltpu.VMEM((SLOTS, CELLS, 128), jnp.bfloat16),
-            pltpu.VMEM((LEVELS, 1, 128), f32),
+            pltpu.VMEM((3, 1, 4), jnp.int32),
             pltpu.VMEM((LEVELS, 128, 128), jnp.bfloat16),
+            pltpu.VMEM((CELLS, 128), f32),
+            pltpu.VMEM((4, PLANES, ORIENT, CELLS), jnp.bfloat16),
             pltpu.VMEM((4, 2, CELLS, 128), f32),
             pltpu.VMEM((256, 256), jnp.bfloat16),
+            pltpu.VMEM((8, 128), f32),
             pltpu.VMEM((2, 4, 2, PLANES, 4, CELLS), f32),
             pltpu.VMEM((4, 2, PLANES, 4, CELLS), f32),
             pltpu.VMEM((ORIENT, CELLS), f32),
@@ -425,16 +449,19 @@
             dma((2, LEVELS)), dma((2, LEVELS)),
             dma((2, 3)), dma((2, 3)),
             dma((2,)), dma((2,)),
-            dma((2,)),
+            dma((9,)),
             dma(()), dma(()),
             dma((3,)), dma((3,)),
             dma(()), dma(()),
         ],
         compiler_params=pltpu.CompilerParams(
-            collective_id=0, has_side_effects=True, vmem_limit_bytes=52 << 20
+            collective_id=0, has_side_effects=True, vmem_limit_bytes=67043328
         ),
         name="chain",
-    )(incoming[0], backward, fields, btr, taps, weights)
+    )(
+        incoming, backward, fields, block_types,
+        axial_taps, lateral_taps, depth_taps, bend_diagonal[None], bend_coupling,
+    )
     return hand[None], den
 
 

time: 93.3 us -> 87.9 us (0.942)
  other arithmetic: 3.32 us -> 0 us
  local copies, waits for them, and re-layouts: 4.57 us -> 2.29 us
    unnamed x11 -> x4, local copies, waits for them, and re-layouts: 4.46 us -> 2.29 us
    div x2 -> x0, other arithmetic: 1.39 us -> none  [the longest x1 0.71 us: per_device(): depth_taps / depth_taps[1]]
where the time goes in v3:
time: 87.9 us; the launch traced here: 87.7 us
  Pallas kernels  84.8 us (96%)
  local copies, waits for them, and re-layouts  2.29 us (3%)
    pallas_call x1, Pallas kernels, per_device(): pl.pallas_call(functools.partial(body, n_gx, contour), out_shape=(jax.Sha...  84.8 us
    unnamed x4, local copies, waits for them, and re-layouts  2.29 us

profile of v3, /device:TPU:9, one launch (start us, length us, event | category | flops | bytes accessed | tf_op | source)
XLA Modules:
  0.0 87.7 jit_solution(3398720392598258364)
XLA Ops:
  0.6 84.8 %chain.1 = (f32[4,64,256]{2,1,0:T(8,128)}, f32[4,4,256]{2,1,0:T(4,128)}) custom-call(f32[1,4,64,256]{3,2,1,0:T(8,128)} %inc_hbm.1, bf16[4,4,64,256]{3,2,1,0:T(8,128)(2,1)} %back.1, f32[3,4,256]{2,1,0:T(4,128)} %fld.1, s32[1,4]{1,0:T(1,128)} %btr_hbm.1, f32[3,64]{1,0:T(4,128)} %ax_hbm.1, f32[3,64]{1,0:T(4,128)} %la_hbm.1, f32[3,64]{1,0:T(4,128)} %de_hbm.1, ...), custom_call_target="tpu_custom_call" | custom-call | tf_op jit(solution)/shard_map/chain/pallas_call | solution.py:413
  85.4 0.0 copy-start
  85.5 1.7 %copy.13 = f32[1,4,64,256]{3,2,1,0:T(8,128)} copy(f32[1,4,64,256]{3,2,1,0:T(8,128)} %bitcast.2) | data formatting | bytes 524288
  87.1 0.0 copy-done
  87.1 0.6 copy.14
Async XLA Ops:
  85.4 1.7 %copy-start = (f32[4,4,256]{2,1,0:T(4,128)S(1)}, f32[4,4,256]{2,1,0:T(4,128)}, u32[]{:S(2)}) copy-start(f32[4,4,256]{2,1,0:T(4,128)} %get-tuple-element.9) | copy-start | bytes 49156

commit v4 on v3

--- a/solution.py
+++ b/solution.py
@@ -22,8 +22,8 @@
     inc_hbm, back, fld, btr_hbm, ax_hbm, la_hbm, de_hbm, diagonal_hbm, coupling_hbm,
     hand, den,
     inc, btr, ax_taps, la_taps, de_taps, diagonal, coupling,
-    lev, q, pad, fw, factors, bt, pick, scaled, held, back_t, wcat, taps, part, summed, relay, r_core, r_y, s_y, r_z,
-    mv_send, mv_recv, mv_extra, relay_sem, h_send, h_recv, f_send, f_recv, b_send, b_recv,
+    lev, q, pad, fw, factors, bt, pick, scaled, along_x, held, back_t, wcat, taps, part, summed, relay, r_core, r_y, s_y, r_z,
+    mv_send, mv_recv, mv_extra, relay_sem, s_send, h_send, h_recv, f_send, f_recv, b_send, b_recv,
     loc, c_send, c_recv, y_send, y_recv, z_send, z_recv,
 ):
     k = lax.axis_index("sec")
@@ -37,6 +37,13 @@
     other_z = lax.rem(k + 8, 16)
     relays = k < 6
     crosses = jnp.logical_and(k >= 6, k <= 7)
+    at_run = lax.rem(g, 8)
+    reach = LEVELS - 8 * (k == 0).astype(jnp.int32) - 4 * (k == 1).astype(jnp.int32)
+    crossed = jnp.logical_and(k >= 8, k <= 9)
+    sends_right = jnp.logical_not(jnp.logical_and(crossed, at_run == 7))
+    sends_left = jnp.logical_not(jnp.logical_and(crossed, at_run == 0))
+    skips_right = jnp.logical_and(crosses, at_run == 7)
+    skips_left = jnp.logical_and(crosses, at_run == 0)
 
     def across(dy):
         return 8 * zhi + 2 * lax.rem(y + dy, 4) + core
@@ -63,6 +70,14 @@
     def _():
         for n in (4, 6):
             pl.semaphore_signal(barrier, inc=1, device_id=(k - n, g), device_id_type=MESH)
+
+        @pl.when(at_run == 0)
+        def _():
+            pl.semaphore_signal(barrier, inc=1, device_id=(k - 2, left), device_id_type=MESH)
+
+        @pl.when(at_run == 7)
+        def _():
+            pl.semaphore_signal(barrier, inc=1, device_id=(k - 2, right), device_id_type=MESH)
 
     for fetch in fetches[:-1]:
         fetch.wait()
@@ -103,11 +118,14 @@
     pair_factor(0, 3, 1, 3, 2)
     pair_factor(1, 3, 0, 3, 3)
 
-    @pl.when(jnp.logical_and(k >= 2, k <= 5))
+    skips = jnp.logical_or(skips_right, skips_left)
+    one_more = jnp.logical_or(jnp.logical_and(k >= 2, k <= 5), skips)
+
+    @pl.when(one_more)
     def _():
         pl.semaphore_wait(barrier, 12)
 
-    @pl.when(jnp.logical_or(k < 2, k > 5))
+    @pl.when(jnp.logical_not(one_more))
     def _():
         pl.semaphore_wait(barrier, 11)
 
@@ -164,6 +182,21 @@
             device_id=(lax.rem(k + ahead, 16), g), device_id_type=MESH,
         )
 
+    def skip_right(p):
+        d = PLANES - p
+        return pltpu.make_async_remote_copy(
+            src_ref=inc.at[p], dst_ref=lev.at[OWN - d], send_sem=s_send.at[p], recv_sem=h_recv.at[0, d - 1],
+            device_id=(k + 2, right), device_id_type=MESH,
+        )
+
+    def skip_left(p):
+        d = p + 1
+        return pltpu.make_async_remote_copy(
+            src_ref=inc.at[p], dst_ref=lev.at[OWN + PLANES - 1 + d], send_sem=s_send.at[p],
+            recv_sem=h_recv.at[1, d - 1],
+            device_id=(k + 2, left), device_id_type=MESH,
+        )
+
     order = (3, 0, 2, 1)
     plain_move = jnp.logical_and(k <= 13, jnp.logical_not(crosses))
 
@@ -172,6 +205,16 @@
         move(3, lax.rem(k + 2, 16), mv_send.at[3], mv_recv.at[3]).start()
         for p in (0, 2, 1):
             to_relay(p).start()
+
+    @pl.when(skips_right)
+    def _():
+        for p in (3, 2, 1, 0):
+            skip_right(p).start()
+
+    @pl.when(skips_left)
+    def _():
+        for p in (0, 1, 2, 3):
+            skip_left(p).start()
 
     @pl.when(plain_move)
     def _():
@@ -195,6 +238,11 @@
 
     field_right(1).start()
     field_left(1).start()
+
+    @pl.when(relays)
+    def _():
+        to_relay(0).wait_recv()
+        from_relay().start()
 
     fetches[-1].wait()
     for j in range(4):
@@ -202,11 +250,6 @@
             both = jnp.concatenate([held[j, p_left], held[j, p_right]], axis=0)
             back_t[j, n] = jnp.transpose(both.astype(jnp.float32))
 
-    @pl.when(relays)
-    def _():
-        to_relay(0).wait_recv()
-        from_relay().start()
-
     def arrive(p):
         @pl.when(k == 0)
         def _():
@@ -216,17 +259,27 @@
         def _():
             move(p, lax.rem(k + 2, 16), mv_send.at[p], mv_recv.at[p]).wait_recv()
 
+    def send_right(d):
+        @pl.when(sends_right)
+        def _():
+            halo_right(d).start()
+
+    def send_left(d):
+        @pl.when(sends_left)
+        def _():
+            halo_left(d).start()
+
     arrive(3)
-    halo_right(1).start()
+    send_right(1)
     arrive(0)
-    halo_left(1).start()
+    send_left(1)
     arrive(2)
-    halo_right(2).start()
+    send_right(2)
     arrive(1)
-    halo_left(2).start()
+    send_left(2)
     for d in (3, 4):
-        halo_right(d).start()
-        halo_left(d).start()
+        send_right(d)
+        send_left(d)
 
     @pl.when(k >= 1)
     def _():
@@ -256,21 +309,19 @@
     load_pair(1, OWN, OWN + 3)
     q[0] = pltpu.roll(q[1], 64, 1)
 
+    ax_out, ax_in, la0, la2, de0, de2 = [taps[pl.ds(n, 1)] for n in range(6)]
+
+    def mix(outer, at):
+        along_x[...] = ax_out * outer + q[at] + ax_in * q[at - 1]
+
     def stage_steps(d, s, carry):
-        restart0 = jnp.logical_and(k == 0, s == 9)
-        restart1 = jnp.logical_and(k == 1, s == 5)
-        level = jnp.where(jnp.logical_or(restart0, restart1), 0, s - 1)
         j = 1 + d - s
-        base = level * SLOTS + j
-        ax_out, ax_in, la0, la2, de0, de2 = [taps[pl.ds(n, 1)] for n in range(6)]
+        at = s * SLOTS + j
         scaled[...] = jnp.dot(factors[j], pick[s - 1], preferred_element_type=jnp.float32)
-        along_x = []
-        for n in range(4):
-            rows = pl.ds(64 * n, 64)
-            along_x.append(ax_out * q[base + 2, rows] + q[base + 1, rows] + ax_in * q[base, rows])
         parts = []
         for n in range(4):
-            b = la0 * along_x[n - 1] + along_x[n] + la2 * along_x[(n + 1) % 4]
+            before, here, after = [along_x[pl.ds(64 * (m % 4), 64)] for m in (n - 1, n, n + 1)]
+            b = la0 * before + here + la2 * after
             pad[n, pl.ds(8, 64)] = b
             pad[n, pl.ds(7, 1)] = b[63:]
             pad[n, pl.ds(72, 1)] = b[:1]
@@ -280,7 +331,14 @@
             parts.append(jnp.concatenate([e_high, e_low], axis=1))
         c = jnp.dot(jnp.concatenate(parts, axis=0), wcat[...], preferred_element_type=jnp.float32)
         fresh = (c[:, :128] + c[:, 128:]) * scaled[...]
-        q[s * SLOTS + j + 1] = fresh
+        mix(fresh, at)
+        q[at + 1] = fresh
+        restart0 = jnp.logical_and(k == 0, s == 8)
+        restart1 = jnp.logical_and(k == 1, s == 4)
+
+        @pl.when(jnp.logical_and(jnp.logical_or(restart0, restart1), j >= 1))
+        def _():
+            mix(q[j + 1], j)
 
         @pl.when(j == 0)
         def _():
@@ -288,18 +346,23 @@
 
         return carry
 
+    mix(q[2], 1)
     stage_steps(0, 1, 0)
 
     def stage(d, carry):
-        halo_right(d).wait_recv()
-
-        @pl.when(d <= LEVELS - PLANES)
+        @pl.when(d <= reach)
+        def _():
+            halo_right(d).wait_recv()
+
+        @pl.when(d <= reach - PLANES)
         def _():
             halo_right(d + PLANES).start()
 
-        halo_left(d).wait_recv()
-
-        @pl.when(d <= LEVELS - PLANES)
+        @pl.when(d <= reach)
+        def _():
+            halo_left(d).wait_recv()
+
+        @pl.when(d <= reach - PLANES)
         def _():
             halo_left(d + PLANES).start()
 
@@ -318,6 +381,7 @@
                 pair_factor(1 + d + n, 3 - r, 3 - n, 3 + r, n)
 
         load_pair(1 + d, OWN - d, OWN + PLANES - 1 + d)
+        mix(q[d + 2], d + 1)
         lax.fori_loop(1, jnp.minimum(d + 1, LEVELS) + 1, functools.partial(stage_steps, d), 0)
         return carry
 
@@ -365,11 +429,17 @@
     to_z.start()
 
     def drain(d, carry):
-        halo_right(d).wait_send()
-        halo_left(d).wait_send()
+        @pl.when(jnp.logical_or(d > PLANES, sends_right))
+        def _():
+            halo_right(d).wait_send()
+
+        @pl.when(jnp.logical_or(d > PLANES, sends_left))
+        def _():
+            halo_left(d).wait_send()
+
         return carry
 
-    lax.fori_loop(1, LEVELS + 1, drain, 0)
+    lax.fori_loop(1, reach + 1, drain, 0)
     for r in (1, 2, 3):
         field_right(r).wait_send()
         field_left(r).wait_send()
@@ -392,6 +462,16 @@
     @pl.when(relays)
     def _():
         from_relay().wait_send()
+
+    @pl.when(skips_right)
+    def _():
+        for p in range(PLANES):
+            skip_right(p).wait_send()
+
+    @pl.when(skips_left)
+    def _():
+        for p in range(PLANES):
+            skip_left(p).wait_send()
 
     to_core.wait_send()
     for dy in (1, 2, 3):
@@ -434,6 +514,7 @@
             pltpu.VMEM((3, 1, 4), jnp.int32),
             pltpu.VMEM((LEVELS, 128, 128), jnp.bfloat16),
             pltpu.VMEM((CELLS, 128), f32),
+            pltpu.VMEM((CELLS, 128), f32),
             pltpu.VMEM((4, PLANES, ORIENT, CELLS), jnp.bfloat16),
             pltpu.VMEM((4, 2, CELLS, 128), f32),
             pltpu.VMEM((256, 256), jnp.bfloat16),
@@ -445,7 +526,7 @@
             pltpu.VMEM((3, 2, PLANES, 4, CELLS), f32),
             pltpu.VMEM((2, PLANES, 4, CELLS), f32),
             pltpu.VMEM((PLANES, 4, CELLS), f32),
-            dma((4,)), dma((4,)), dma((4,)), dma((2,)),
+            dma((4,)), dma((4,)), dma((4,)), dma((2,)), dma((4,)),
             dma((2, LEVELS)), dma((2, LEVELS)),
             dma((2, 3)), dma((2, 3)),
             dma((2,)), dma((2,)),

time: 87.9 us -> 85.1 us (0.968)
  the two profiles are of different devices: /device:TPU:9 before, /device:TPU:1 now
where the time goes in v4:
time: 85.1 us; the launch traced here: 84.9 us
  Pallas kernels  82 us (96%)
  local copies, waits for them, and re-layouts  2.29 us (3%)
    pallas_call x1, Pallas kernels, per_device(): pl.pallas_call(functools.partial(body, n_gx, contour), out_shape=(jax.Sha...  82 us
    unnamed x4, local copies, waits for them, and re-layouts  2.29 us

profile of v4, /device:TPU:1, one launch (start us, length us, event | category | flops | bytes accessed | tf_op | source)
XLA Modules:
  0.0 84.9 jit_solution(13113156465122959363)
XLA Ops:
  0.6 82.0 %chain.1 = (f32[4,64,256]{2,1,0:T(8,128)}, f32[4,4,256]{2,1,0:T(4,128)}) custom-call(f32[1,4,64,256]{3,2,1,0:T(8,128)} %inc_hbm.1, bf16[4,4,64,256]{3,2,1,0:T(8,128)(2,1)} %back.1, f32[3,4,256]{2,1,0:T(4,128)} %fld.1, s32[1,4]{1,0:T(1,128)} %btr_hbm.1, f32[3,64]{1,0:T(4,128)} %ax_hbm.1, f32[3,64]{1,0:T(4,128)} %la_hbm.1, f32[3,64]{1,0:T(4,128)} %de_hbm.1, ...), custom_call_target="tpu_custom_call" | custom-call | tf_op jit(solution)/shard_map/chain/pallas_call | solution.py:493
  82.7 0.0 copy-start
  82.7 1.7 %copy.13 = f32[1,4,64,256]{3,2,1,0:T(8,128)} copy(f32[1,4,64,256]{3,2,1,0:T(8,128)} %bitcast.2) | data formatting | bytes 524288
  84.3 0.0 copy-done
  84.3 0.6 copy.14
Async XLA Ops:
  82.7 1.7 %copy-start = (f32[4,4,256]{2,1,0:T(4,128)S(1)}, f32[4,4,256]{2,1,0:T(4,128)}, u32[]{:S(2)}) copy-start(f32[4,4,256]{2,1,0:T(4,128)} %get-tuple-element.9) | copy-start | bytes 49156
